TPU v7x, 32 devices: a whole 2x2x4 slice. The times are simulated.
32 devices in a mesh: dp: 8 (over z, x), ctx: 4 (over y, core).
Axes of the slice: x: 2, y: 2, z: 4, core: 2. Of those that a mesh axis runs over, the one named last changes fastest.
Arguments:
- tokens: bfloat16 [16, 2048, 768], P('dp', 'ctx'), may hold values from -6 to 6
- segments: int32 [16, 2048], P('dp'), may hold values from 0 to 4, never falling along the last dimension, each value on 1 to 800 neighbouring positions
- cotangent: bfloat16 [16, 2048, 768], P('dp', 'ctx'), may hold values from -6 to 6
- query_weight: bfloat16 [768, 768], P(('dp', 'ctx')), may hold values from -0.21875 to 0.21875
- query_bias: bfloat16 [768], P(('dp', 'ctx')), may hold values from -3 to 3
- key_weight: bfloat16 [768, 768], P(('dp', 'ctx')), may hold values from -0.21875 to 0.21875
- value_weight: bfloat16 [768, 768], P(('dp', 'ctx')), may hold values from -0.21875 to 0.21875
- value_bias: bfloat16 [768], P(('dp', 'ctx')), may hold values from -0.59765625 to 0.59765625
- output_weight: bfloat16 [768, 768], P(('dp', 'ctx')), may hold values from -0.875 to 0.875
- output_bias: bfloat16 [768], P(('dp', 'ctx')), may hold values from -2 to 2
- first_gain: bfloat16 [768], P(('dp', 'ctx')), may hold values from 0.5 to 1.5
- first_shift: bfloat16 [768], P(('dp', 'ctx')), may hold values from -2 to 2
- inner_weight: bfloat16 [768, 3072], P(('dp', 'ctx')), may hold values from -0.21875 to 0.21875
- inner_bias: bfloat16 [3072], P(('dp', 'ctx')), may hold values from -3 to 3
- outer_weight: bfloat16 [3072, 768], P(('dp', 'ctx')), may hold values from -0.109375 to 0.109375
- outer_bias: bfloat16 [768], P(('dp', 'ctx')), may hold values from -2 to 2
- second_gain: bfloat16 [768], P(('dp', 'ctx')), may hold values from 0.5 to 1.5
- second_shift: bfloat16 [768], P(('dp', 'ctx')), may hold values from -2 to 2
Outputs:
- layer_output: bfloat16 [16, 2048, 768], P('dp', 'ctx')
- input_gradient: float32 [16, 2048, 768], P('dp', 'ctx')
- query_weight_gradient: float32 [768, 768], P(('dp', 'ctx'))
- query_bias_gradient: float32 [768], P(('dp', 'ctx'))
- key_weight_gradient: float32 [768, 768], P(('dp', 'ctx'))
- value_weight_gradient: float32 [768, 768], P(('dp', 'ctx'))
- value_bias_gradient: float32 [768], P(('dp', 'ctx'))
- output_weight_gradient: float32 [768, 768], P(('dp', 'ctx'))
- output_bias_gradient: float32 [768], P(('dp', 'ctx'))
- first_gain_gradient: float32 [768], P(('dp', 'ctx'))
- first_shift_gradient: float32 [768], P(('dp', 'ctx'))
- inner_weight_gradient: float32 [768, 3072], P(('dp', 'ctx'))
- inner_bias_gradient: float32 [3072], P(('dp', 'ctx'))
- outer_weight_gradient: float32 [3072, 768], P(('dp', 'ctx'))
- outer_bias_gradient: float32 [768], P(('dp', 'ctx'))
- second_gain_gradient: float32 [768], P(('dp', 'ctx'))
- second_shift_gradient: float32 [768], P(('dp', 'ctx'))
Inputs may be any that keep to these rules, and one draw needn't show every extreme that they name: `segments`: in each sequence the document numbers start at 0 and never fall; a document has 1 to 800 tokens, one of each sequence exactly 800, and there are at most 5 documents.
All inputs are finite; a program needn't handle non-finite values.
Results may differ from a plain program's by a relative error of at most 0.028.
Values may be sent and summed in bfloat16 or wider, within the bound.
No kernel may reach another device: no remote copies, remote signals or barrier semaphores. Data moves between devices by JAX's collectives and lax.ppermute only.
A program may use at most 384 MiB of HBM per device.

v0:
```python
import functools
import math

import jax
import jax.numpy as jnp
from jax import lax
from jax.experimental import pallas as pl
from jax.experimental.pallas import tpu as pltpu
from jax.sharding import Mesh
from jax.sharding import PartitionSpec as P

from jax.sharding import Mesh
from jax.sharding import PartitionSpec as P

HEAD = 64
PAIR = 2 * HEAD
BQ = 256
BK = 256
LOG2E = math.log2(math.e)
epsilon = 1e-05
f32 = jnp.float32
bf16 = jnp.bfloat16


def dot(left, right):
    return jnp.dot(left, right, preferred_element_type=f32)


def lanes_of(shape, head):
    lane = lax.broadcasted_iota(jnp.int32, shape, 1)
    return (lane < HEAD) if head == 0 else (lane >= HEAD)


def rows_of(shape, head):
    row = lax.broadcasted_iota(jnp.int32, shape, 0)
    return (row < HEAD) if head == 0 else (row >= HEAD)


def attend_kernel(lo, hi, q_ref, k_ref, v_ref, seg_col_ref, seg_row_ref, o_ref, lse_ref, kt_ref, v_scr, *, base):
    step = pl.program_id(0)
    group = q_ref.shape[1] // PAIR
    heads = [(p, h) for p in range(group) for h in (0, 1)]
    at_pair = [slice(p * PAIR, (p + 1) * PAIR) for p in range(group)]

    @pl.when(step == 0)
    def _():
        for p in range(group):
            kt_ref[at_pair[p], :] = k_ref[:, at_pair[p]].astype(f32).T.astype(bf16)
            values = v_ref[:, at_pair[p]].astype(f32)
            for h in (0, 1):
                v_scr[2 * p + h] = jnp.where(lanes_of(values.shape, h), values, 1.0).astype(bf16)

    split = []
    for p in range(group):
        queries = q_ref[:, at_pair[p]].astype(f32)
        split += [jnp.where(lanes_of(queries.shape, h), queries, 0.0).astype(bf16) for h in (0, 1)]
    seg_q = seg_col_ref[:, 0:1]

    def one(block, carry):
        at = pl.multiple_of(block * BK, BK)
        allowed = seg_q == seg_row_ref[0:1, pl.ds(at, BK)]
        out = []
        for n, (p, h) in enumerate(heads):
            peak, acc = carry[2 * n], carry[2 * n + 1]
            scores = dot(split[n], kt_ref[at_pair[p], pl.ds(at, BK)])
            scores = jnp.where(allowed, scores * (LOG2E / math.sqrt(HEAD)), -1e30)
            top = jnp.maximum(peak, jnp.max(scores, axis=1, keepdims=True))
            probs = jnp.exp2(scores - top)
            acc = acc * jnp.exp2(peak - top) + dot(probs.astype(bf16), v_scr[n, pl.ds(at, BK), :])
            out += [top, acc]
        return tuple(out)

    start = (jnp.full((BQ, 1), -1e30, f32), jnp.zeros((BQ, PAIR), f32)) * len(heads)
    done = lax.fori_loop(lo[base + step], hi[base + step], one, start)
    for p in range(group):
        peak0, acc0, peak1, acc1 = done[4 * p : 4 * p + 4]
        sums0 = pltpu.roll(acc0, HEAD, 1)
        sums1 = pltpu.roll(acc1, HEAD, 1)
        first = lanes_of(acc0.shape, 0)
        o_ref[:, at_pair[p]] = (jnp.where(first, acc0, acc1) / jnp.where(first, sums0, sums1)).astype(bf16)
        logs = jnp.where(first, peak1 + jnp.log2(acc1), peak0 + jnp.log2(acc0)).T
        lse_ref[16 * p : 16 * p + 8, :] = logs[HEAD : HEAD + 8, :]
        lse_ref[16 * p + 8 : 16 * p + 16, :] = logs[0:8, :]


def attend_back_kernel(
    lo, hi, q_ref, k_ref, v_ref, do_ref, o_ref, lse_ref, seg_row_ref, seg_col_ref, *refs, base, last
):
    if last:
        dk_before, dv_before, dq_ref, dk_ref, dv_ref, kt_ref, dk_acc, dv_acc = refs
    else:
        dq_ref, dk_acc, dv_acc, kt_ref = refs
    step = pl.program_id(0)
    group = q_ref.shape[1] // PAIR
    at_pair = [slice(p * PAIR, (p + 1) * PAIR) for p in range(group)]

    @pl.when(step == 0)
    def _():
        for p in range(group):
            kt_ref[at_pair[p], :] = k_ref[:, at_pair[p]].astype(f32).T.astype(bf16)
        dk_acc[...] = dk_before[...] if last else jnp.zeros_like(dk_acc)
        dv_acc[...] = dv_before[...] if last else jnp.zeros_like(dv_acc)

    q_rows, g_rows, q_cols, g_cols, mean, logs = [], [], [], [], [], []
    for p in range(group):
        queries = q_ref[:, at_pair[p]].astype(f32)
        grads = do_ref[:, at_pair[p]].astype(f32)
        queries_t = queries.T
        grads_t = grads.T
        inner_t = grads_t * o_ref[:, at_pair[p]].astype(f32).T
        for h in (0, 1):
            q_rows.append(jnp.where(lanes_of(queries.shape, h), queries, 0.0).astype(bf16))
            g_rows.append(jnp.where(lanes_of(grads.shape, h), grads, 0.0).astype(bf16))
            q_cols.append(jnp.where(rows_of(queries_t.shape, h), queries_t, 0.0).astype(bf16))
            g_cols.append(jnp.where(rows_of(grads_t.shape, h), grads_t, 0.0).astype(bf16))
            mean.append(jnp.sum(inner_t[h * HEAD : (h + 1) * HEAD, :], axis=0, keepdims=True))
            logs.append(lse_ref[16 * p + 8 * h : 16 * p + 8 * h + 1, :])
    seg_q = seg_row_ref[0:1, :]

    def one(block, carry):
        at = pl.multiple_of(block * BK, BK)
        allowed = seg_col_ref[pl.ds(at, BK), 0:1] == seg_q
        out = []
        for p in range(group):
            keys = k_ref[pl.ds(at, BK), at_pair[p]]
            values = v_ref[pl.ds(at, BK), at_pair[p]]
            probs, scores_grad = [], []
            for h in (0, 1):
                n = 2 * p + h
                scores = dot(keys, q_cols[n]) * (LOG2E / math.sqrt(HEAD)) - logs[n]
                weight = jnp.exp2(jnp.where(allowed, scores, -1e30))
                ds = (weight * (dot(values, g_cols[n]) - mean[n])).astype(bf16)
                probs.append(weight.astype(bf16))
                scores_grad.append(ds)
                rows = slice(p * PAIR + h * HEAD, p * PAIR + (h + 1) * HEAD)
                out.append(carry[n] + dot(kt_ref[rows, pl.ds(at, BK)], ds))
            n = 2 * p
            dv_acc[pl.ds(at, BK), at_pair[p]] += dot(probs[0], g_rows[n]) + dot(probs[1], g_rows[n + 1])
            dk_acc[pl.ds(at, BK), at_pair[p]] += dot(scores_grad[0], q_rows[n]) + dot(scores_grad[1], q_rows[n + 1])
        return tuple(out)

    start = (jnp.zeros((HEAD, BQ), f32),) * (2 * group)
    done = lax.fori_loop(lo[base + step], hi[base + step], one, start)
    for p in range(group):
        turned = jnp.concatenate([done[2 * p], done[2 * p + 1]], axis=0).T
        dq_ref[:, at_pair[p]] = (turned * (1.0 / math.sqrt(HEAD))).astype(bf16)

    if not last:
        return

    @pl.when(step == pl.num_programs(0) - 1)
    def _():
        dk_ref[...] = (dk_acc[...] * (1.0 / math.sqrt(HEAD))).astype(bf16)
        dv_ref[...] = dv_acc[...].astype(bf16)


def key_range(seg):
    blocks = seg.reshape(-1, BQ)
    first = jnp.sum(seg[None, :] < blocks[:, :1], axis=1, dtype=jnp.int32)
    last = jnp.sum(seg[None, :] <= blocks[:, -1:], axis=1, dtype=jnp.int32)
    return first // BK, (last + BK - 1) // BK


def attend(qkv, base, count, seg_row, seg_col, lo, hi):
    length, wide = qkv.shape
    half = wide // 3
    whole = lambda part: pl.BlockSpec((length, half), lambda i, lo, hi: (0, part))
    return pl.pallas_call(
        functools.partial(attend_kernel, base=base),
        out_shape=(
            jax.ShapeDtypeStruct((count * BQ, half), bf16),
            jax.ShapeDtypeStruct((half // PAIR * 16, count * BQ), f32),
        ),
        grid_spec=pltpu.PrefetchScalarGridSpec(
            num_scalar_prefetch=2,
            grid=(count,),
            in_specs=[
                pl.BlockSpec((BQ, half), lambda i, lo, hi: (base + i, 0)),
                whole(1),
                whole(2),
                pl.BlockSpec((BQ, PAIR), lambda i, lo, hi: (base + i, 0)),
                pl.BlockSpec((8, length), lambda i, lo, hi: (0, 0)),
            ],
            out_specs=[
                pl.BlockSpec((BQ, half), lambda i, lo, hi: (i, 0)),
                pl.BlockSpec((half // PAIR * 16, BQ), lambda i, lo, hi: (0, i)),
            ],
            scratch_shapes=[
                pltpu.VMEM((half, length), bf16),
                pltpu.VMEM((half // HEAD, length, PAIR), bf16),
            ],
        ),
        compiler_params=pltpu.CompilerParams(dimension_semantics=("arbitrary",)),
        name="attend",
    )(lo, hi, qkv, qkv, qkv, seg_col, seg_row)


def attend_back(qkv, base, count, before, mixed, d_mixed, lse, seg_row, seg_col, lo, hi):
    length, wide = qkv.shape
    half = wide // 3
    whole = lambda part: pl.BlockSpec((length, half), lambda i, lo, hi: (0, part))
    rows = pl.BlockSpec((BQ, half), lambda i, lo, hi: (base + i, 0))
    last = bool(before)
    kind = bf16 if last else f32
    return pl.pallas_call(
        functools.partial(attend_back_kernel, base=base, last=last),
        out_shape=(
            jax.ShapeDtypeStruct((count * BQ, half), bf16),
            jax.ShapeDtypeStruct((length, half), kind),
            jax.ShapeDtypeStruct((length, half), kind),
        ),
        grid_spec=pltpu.PrefetchScalarGridSpec(
            num_scalar_prefetch=2,
            grid=(count,),
            in_specs=[
                rows,
                whole(1),
                whole(2),
                rows,
                rows,
                pl.BlockSpec((half // PAIR * 16, BQ), lambda i, lo, hi: (0, base + i)),
                pl.BlockSpec((8, BQ), lambda i, lo, hi: (0, base + i)),
                pl.BlockSpec((length, PAIR), lambda i, lo, hi: (0, 0)),
            ]
            + [whole(0)] * len(before),
            out_specs=[pl.BlockSpec((BQ, half), lambda i, lo, hi: (i, 0)), whole(0), whole(0)],
            scratch_shapes=[pltpu.VMEM((half, length), bf16)] + [pltpu.VMEM((length, half), f32)] * (2 * last),
        ),
        compiler_params=pltpu.CompilerParams(dimension_semantics=("arbitrary",)),
        name="attend_back",
    )(lo, hi, qkv, qkv, qkv, d_mixed, mixed, lse, seg_row, seg_col, *before)


def bit_of(name):
    axis, step = name
    return (lax.axis_index(axis) // step) % 2


def swap(values, name):
    axis, step = name
    count = lax.axis_size(axis)
    return lax.ppermute(values, axis, [(i, i ^ step) for i in range(count)])


def pick(values, index, dim):
    return lax.dynamic_index_in_dim(values, index, dim, keepdims=False)


def in_order(bit, mine, other, dim=0):
    low = jnp.where(bit == 0, mine, other)
    high = jnp.where(bit == 0, other, mine)
    return jnp.stack([low, high], axis=dim)


def grow(values, names):
    for name in names:
        got = swap(values, name)
        values = in_order(bit_of(name), values, got)
    return values


def sort_blocks(values, names, wanted):
    stacked = list(reversed(names))
    order = [stacked.index(name) for name in wanted]
    count = len(names)
    return values.transpose(order + list(range(count, values.ndim)))


def shrink(values, names, wanted):
    left = list(wanted)
    for name in names:
        dim = left.index(name)
        bit = bit_of(name)
        got = swap(pick(values, 1 - bit, dim), name)
        values = pick(values, bit, dim).astype(f32) + got.astype(f32)
        left.remove(name)
        if left:
            values = values.astype(bf16)
    return values


def norm_stats(values):
    average = jnp.mean(values, axis=-1, keepdims=True)
    centred = values - average
    spread = jnp.mean(centred * centred, axis=-1, keepdims=True)
    inverse = lax.rsqrt(spread + epsilon)
    return centred * inverse, inverse


def norm_back(grad, gain, unit, inverse):
    u = grad * gain
    first = jnp.mean(u, axis=-1, keepdims=True)
    second = jnp.mean(u * unit, axis=-1, keepdims=True)
    return (u - first - unit * second) * inverse


def dot_rows(left, right):
    return lax.dot_general(left, right, (((0,), (0,)), ((), ())), preferred_element_type=f32)


def dot_cols(left, right):
    return lax.dot_general(left, right, (((1,), (1,)), ((), ())), preferred_element_type=f32)


def column_sums(values):
    return jnp.sum(values.astype(f32), axis=0)


def on_device(
    tokens, segments, cotangent, query_weight, query_bias, key_weight, value_weight, value_bias,
    output_weight, output_bias, first_gain, first_shift, inner_weight, inner_bias, outer_weight,
    outer_bias, second_gain, second_shift,
):
    core = ("c", 1)
    partner = ("y", 1)
    y = bit_of(partner)
    c = bit_of(core)
    local, width = tokens.shape[1], tokens.shape[2]
    own, hidden = inner_weight.shape
    half = width // 2
    length = segments.shape[1]
    chunks = hidden // width
    bits = lambda axis: [(axis, 1 << k) for k in reversed(range(lax.axis_size(axis).bit_length() - 1))]
    y_names = bits("y")
    far, near = bits("dp")[:-1], bits("dp")[-1]
    wanted = bits("dp") + y_names
    team = y_names[:-1]
    rank = lax.axis_index("y") // 2
    blocks = (2,) * len(wanted)

    columns = jnp.stack(
        [query_bias, value_bias, output_bias, first_gain, first_shift, outer_bias, second_gain, second_shift],
        axis=1,
    )
    columns = jnp.concatenate([columns, inner_bias.reshape(own, chunks)], axis=1)
    columns = jnp.pad(columns, ((0, 0), (0, PAIR - columns.shape[1])))

    def three(index):
        return jnp.concatenate(
            [lax.dynamic_slice_in_dim(w, index * half, half, 1) for w in (query_weight, key_weight, value_weight)]
            + [columns],
            axis=1,
        )

    attention_part = in_order(c, three(c), swap(three(1 - c), core)).reshape(2 * own, 3 * half + PAIR)

    def to_chip(values):
        return in_order(y, pick(values, y, 0), swap(pick(values, 1 - y, 0), partner))

    mine = to_chip(tokens)
    source_all = grow(in_order(c, mine, swap(mine, core), 1), team).reshape(length, width)
    source = mine.reshape(2 * local, width)

    attention_part = grow(attention_part, far)
    cut = (3 * half + PAIR) // 2 // 128 * 128
    output_inner = jnp.concatenate([output_weight, inner_weight], axis=1)
    output_inner, outer_part, attention_part = lax.optimization_barrier((output_inner, outer_weight, attention_part))
    part_a = grow(attention_part[..., :cut], [near] + y_names)
    part_b = grow(attention_part[..., cut:], y_names + [near])
    part_a = sort_blocks(part_a, far + [near] + y_names, wanted).reshape(width, cut)
    part_b = sort_blocks(part_b, far + y_names + [near], wanted).reshape(width, 3 * half + PAIR - cut)
    joined = jnp.concatenate([part_a, part_b], axis=1)
    qkv_weight = joined[:, : 3 * half]
    vectors = joined[:, 3 * half :].astype(f32).T
    half_of = lambda row: lax.dynamic_slice_in_dim(row, c * half, half, 0)
    qkv_bias = jnp.concatenate([half_of(vectors[0]), jnp.zeros((half,), f32), half_of(vectors[1])])
    output_bias, first_gain, first_shift, outer_bias, second_gain, second_shift = [vectors[k] for k in range(2, 8)]
    inner_bias = joined[:, 3 * half + 8 : 3 * half + 8 + chunks].reshape(hidden).astype(f32)

    output_inner = grow(output_inner, far)
    outer_part = grow(outer_part, far)
    output_inner = sort_blocks(grow(output_inner, [near] + y_names), far + [near] + y_names, wanted)
    outer_part = sort_blocks(grow(outer_part, y_names + [near]), far + y_names + [near], wanted)
    output_inner = in_order(c, output_inner, swap(output_inner, core), len(wanted)).reshape(width, width + hidden)
    outer_weight = in_order(c, outer_part, swap(outer_part, core), len(wanted)).reshape(hidden, width)
    output_weight = output_inner[:, :width]
    inner_weight = output_inner[:, width:]

    seg = pick(segments, y, 0)
    lo, hi = key_range(seg)
    seg_row = jnp.broadcast_to(seg[None, :], (8, length))
    seg_col = jnp.broadcast_to(seg[:, None], (length, PAIR))
    qkv = (dot(source_all, qkv_weight) + qkv_bias).astype(bf16)
    attended = []
    steps = length // BQ
    marks = [0, (3 * steps + 7) // 8, (6 * steps + 7) // 8, steps]
    for p in range(3):
        attended.append(attend(qkv, marks[p], marks[p + 1] - marks[p], seg_row, seg_col, lo, hi))
    mixed_all = jnp.concatenate([a[0] for a in attended], axis=0)
    log_sums = jnp.concatenate([a[1] for a in attended], axis=1)
    mixed_heads = pick(mixed_all.reshape(-1, 2, 2, local, half), rank, 0)
    got = swap(pick(mixed_heads, 1 - c, 1), core)
    mixed = in_order(c, pick(mixed_heads, c, 1), got, 2).reshape(2 * local, width)

    pre = source.astype(f32) + dot(mixed, output_weight) + output_bias
    first_unit, first_inverse = norm_stats(pre)
    first = first_unit * first_gain + first_shift
    first_low = first.astype(bf16)
    inner = dot(first_low, inner_weight) + inner_bias
    phi = 0.5 * (1.0 + lax.erf(inner * math.sqrt(0.5)))
    active = (inner * phi).astype(bf16)
    slope = (phi + inner * (jnp.exp(-0.5 * inner * inner) * (1.0 / math.sqrt(2.0 * math.pi)))).astype(bf16)
    total = first + dot(active, outer_weight) + outer_bias
    second_unit, second_inverse = norm_stats(total)
    result = (second_unit * second_gain + second_shift).astype(bf16).reshape(2, local, width)

    def to_owner(values):
        kept = pick(values, y, 0)
        return in_order(y, kept, swap(pick(values, 1 - y, 0).astype(bf16), partner).astype(kept.dtype))

    layer_output = to_owner(result)

    grad = to_chip(cotangent).reshape(2 * local, width).astype(f32)
    d_total = norm_back(grad, second_gain, second_unit, second_inverse)
    d_second_gain = jnp.sum(grad * second_unit, axis=0)
    d_second_shift = jnp.sum(grad, axis=0)
    d_outer = d_total.astype(bf16)

    def core_then_chips(gradient, names):
        gradient = gradient.astype(bf16)
        rows, cols = gradient.shape
        shaped = gradient.reshape(blocks + (2, rows // (2 * math.prod(blocks)), cols))
        dim = len(wanted)
        got = swap(pick(shaped, 1 - c, dim), core)
        summed = (pick(shaped, c, dim).astype(f32) + got.astype(f32)).astype(bf16)
        return shrink(summed, names, wanted)

    back = list(reversed(far))
    g_outer_weight = core_then_chips(dot_rows(active, d_outer), [near] + y_names + back)
    d_inner = (dot_cols(d_outer, outer_weight) * slope.astype(f32)).astype(bf16)
    g_inner_weight = core_then_chips(dot_rows(first_low, d_inner), y_names + [near] + back)
    d_first = dot_cols(d_inner, inner_weight) + d_total
    d_pre = norm_back(d_first, first_gain, first_unit, first_inverse)
    d_attended = d_pre.astype(bf16)
    d_mixed = dot_cols(d_attended, output_weight).astype(bf16)
    d_mixed = d_mixed.reshape(2 * local, 2, half)
    got = swap(pick(d_mixed, 1 - c, 1), core)
    d_heads = in_order(c, pick(d_mixed, c, 1).reshape(2, local, half), got.reshape(2, local, half), 1)
    d_heads = grow(d_heads, reversed(team)).reshape(length, half)

    g_columns = jnp.stack(
        [
            column_sums(d_attended),
            jnp.sum(d_first * first_unit, axis=0),
            jnp.sum(d_first, axis=0),
            column_sums(d_outer),
            d_second_gain,
            d_second_shift,
        ],
        axis=1,
    )
    g_columns = jnp.concatenate([g_columns, column_sums(d_inner).reshape(width, chunks)], axis=1)
    g_columns = jnp.pad(g_columns, ((0, 0), (0, PAIR - g_columns.shape[1])))
    g_output = core_then_chips(
        jnp.concatenate([dot_rows(mixed, d_attended), g_columns], axis=1), y_names + [near] + back
    )

    part = attend_back(qkv, 0, steps // 2, (), mixed_all, d_heads, log_sums, seg_row, seg_col, lo, hi)
    rest = attend_back(
        qkv, steps // 2, steps - steps // 2, part[1:], mixed_all, d_heads, log_sums, seg_row, seg_col, lo, hi
    )
    d_qkv = jnp.concatenate([jnp.concatenate([part[0], rest[0]], axis=0), rest[1], rest[2]], axis=1)
    place = lambda part: lax.dynamic_update_slice_in_dim(
        jnp.zeros((width,), f32), column_sums(d_qkv[:, part * half : (part + 1) * half]), c * half, 0
    )
    g_bias = jnp.pad(jnp.stack([place(0), place(2)], axis=1), ((0, 0), (0, PAIR - 2)))
    g_qkv = dot_rows(source_all, d_qkv)
    g_qkv = jnp.concatenate([g_qkv, g_bias], axis=1).astype(bf16)
    if team:
        g_qkv = jnp.where(rank == 0, g_qkv, jnp.zeros_like(g_qkv))
    g_qkv = g_qkv.reshape(blocks + (2 * own, 3 * half + PAIR))
    g_a = shrink(g_qkv[..., :cut], y_names + [near] + back, wanted)
    g_b = shrink(g_qkv[..., cut:], [near] + y_names + back, wanted)
    g_chip = jnp.concatenate([g_a, g_b], axis=1).reshape(2, own, 3 * half + PAIR)
    kept = pick(g_chip, c, 0)
    got = swap(pick(g_chip, 1 - c, 0), core)
    g_weights = in_order(c, kept[:, : 3 * half], got[:, : 3 * half])
    g_biases = kept[:, 3 * half :] + got[:, 3 * half :]
    g_three = [
        jnp.concatenate([g_weights[0, :, k * half : (k + 1) * half], g_weights[1, :, k * half : (k + 1) * half]], axis=1)
        for k in range(3)
    ]

    shaped = pick(d_qkv.reshape(-1, 2, 2, local, 3 * half), rank, 0)
    other = dot_cols(pick(shaped, 1 - c, 1).reshape(2 * local, 3 * half), qkv_weight).astype(bf16)
    other = swap(other, core)
    d_input = d_pre + dot_cols(pick(shaped, c, 1).reshape(2 * local, 3 * half), qkv_weight) + other.astype(f32)
    input_gradient = to_owner(d_input.reshape(2, local, width))

    return (
        layer_output,
        input_gradient,
        g_three[0],
        g_biases[:, 0],
        g_three[1],
        g_three[2],
        g_biases[:, 1],
        g_output[:, :width],
        g_output[:, width],
        g_output[:, width + 1],
        g_output[:, width + 2],
        g_inner_weight,
        g_output[:, width + 6 : width + 6 + chunks].reshape(own * chunks),
        g_outer_weight,
        g_output[:, width + 3],
        g_output[:, width + 4],
        g_output[:, width + 5],
    )


def solution(mesh):
    dp, ctx = mesh.shape["dp"], mesh.shape["ctx"]
    split = Mesh(mesh.devices.reshape(dp, ctx // 2, 2), ("dp", "y", "c"))
    every = ("dp", "y", "c")
    tokens = P("dp", ("y", "c"), None)
    matrix = P(every, None)
    vector = P(every)

    return jax.shard_map(
        on_device,
        mesh=split,
        in_specs=(
            tokens, P("dp", None), tokens,
            matrix, vector, matrix, matrix, vector, matrix, vector, vector, vector,
            matrix, vector, matrix, vector, vector, vector,
        ),
        out_specs=(
            tokens, tokens,
            matrix, vector, matrix, matrix, vector, matrix, vector, vector, vector,
            matrix, vector, matrix, vector, vector, vector,
        ),
        check_vma=False,
    )
```

profile of v0, /device:TPU:0, one launch (start us, length us, event | category | flops | bytes accessed | tf_op | source)
XLA Modules:
  0.0 570.0 jit_solution(14827735811629917090)
XLA Ops:
  28.6 6.0 %collective-permute-done.4 = bf16[2,48,1280]{2,1,0:T(8,128)(2,1)} collective-permute-done((bf16[2,48,1280]{2,1,0:T(8,128)(2,1)}, bf16[2,48,1280]{2,1,0:T(8,128)(2,1)}, u32[]{:S(2)}, u32[]{:S(2)}) %collective-permute-start.4) | collective-permute-done | bytes 245792 | tf_op jit(solution)/shard_map/ppermute | solution.py:242
  46.6 9.5 %collective-permute-done.10 = bf16[24,3840]{1,0:T(8,128)(2,1)S(1)} collective-permute-done((bf16[24,3840]{1,0:T(8,128)(2,1)S(1)}, bf16[24,3840]{1,0:T(8,128)(2,1)S(1)}, u32[]{:S(2)}, u32[]{:S(2)}) %collective-permute-start.10) | collective-permute-done | bytes 184352 | tf_op jit(solution)/shard_map/ppermute | solution.py:242
  74.9 7.1 %collective-permute-done.17 = bf16[2,2,96,768]{3,2,0,1:T(8,128)(2,1)S(1)} collective-permute-done((bf16[2,2,96,768]{3,2,0,1:T(8,128)(2,1)S(1)}, bf16[2,2,96,768]{3,2,0,1:T(8,128)(2,1)S(1)}, u32[]{:S(2)}, u32[]{:S(2)}) %collective-permute-start.17) | collective-permute-done | bytes 589856 | tf_op jit(solution)/shard_map/ppermute | solution.py:242
  83.8 7.0 %collective-permute-done.12 = bf16[2,2,24,3840]{3,2,0,1:T(8,128)(2,1)S(1)} collective-permute-done((bf16[2,2,24,3840]{3,2,0,1:T(8,128)(2,1)S(1)}, bf16[2,2,24,3840]{3,2,0,1:T(8,128)(2,1)S(1)}, u32[]{:S(2)}, u32[]{:S(2)}) %collective-permute-start.12) | collective-permute-done | bytes 737312 | tf_op jit(solution)/shard_map/ppermute | solution.py:242
  93.5 19.1 %collective-permute-done.18 = bf16[2,2,2,96,768]{4,3,0,1,2:T(8,128)(2,1)S(1)} collective-permute-done((bf16[2,2,2,96,768]{4,3,0,1,2:T(8,128)(2,1)S(1)}, bf16[2,2,2,96,768]{4,3,0,1,2:T(8,128)(2,1)S(1)}, u32[]{:S(2)}, u32[]{:S(2)}) %collective-permute-start.18) | collective-permute-done | bytes 1179680 | tf_op jit(solution)/shard_map/ppermute | solution.py:242
  120.8 6.4 %add_convert_fusion.q_ref.k_ref.v_ref = bf16[2048,1152]{1,0:T(8,128)(2,1)} fusion(bf16[2048,768]{1,0:T(8,128)(2,1)S(1)} %bitcast.424, f32[1152]{0:T(1024)S(1)} %pad_maximum_fusion.31, bf16[768,640]{1,0:T(8,128)(2,1)S(1)} %bitcast.448, bf16[768,640]{1,0:T(8,128)(2,1)S(1)} %bitcast.461), kind=kOutput, calls=%fused_computation.9 | convolution fusion | flops 3632136192 | bytes 9835008 | tf_op jit(solution)/shard_map/dot_general | solution.py:26
  129.3 19.9 %attend.4 = (bf16[768,384]{1,0:T(8,128)(2,1)}, f32[48,768]{1,0:T(8,128)}) custom-call(s32[8]{0:T(128)} %get-tuple-element.170.lo, s32[8]{0:T(128)} %get-tuple-element.169.hi, bf16[2048,1152]{1,0:T(8,128)(2,1)} %add_convert_fusion.q_ref.k_ref.v_ref, bf16[2048,1152]{1,0:T(8,128)(2,1)} %add_convert_fusion.q_ref.k_ref.v_ref, ...), custom_call_target="tpu_custom_call" | custom-call | tf_op jit(solution)/shard_map/attend/pallas_call | solution.py:168
  149.1 17.7 %attend.3 = (bf16[768,384]{1,0:T(8,128)(2,1)}, f32[48,768]{1,0:T(8,128)}) custom-call(s32[8]{0:T(128)} %get-tuple-element.170.lo, s32[8]{0:T(128)} %get-tuple-element.169.hi, bf16[2048,1152]{1,0:T(8,128)(2,1)} %add_convert_fusion.q_ref.k_ref.v_ref, bf16[2048,1152]{1,0:T(8,128)(2,1)} %add_convert_fusion.q_ref.k_ref.v_ref, ...), custom_call_target="tpu_custom_call" | custom-call | tf_op jit(solution)/shard_map/attend/pallas_call | solution.py:168
  166.8 15.0 %attend.5 = (bf16[512,384]{1,0:T(8,128)(2,1)}, f32[48,512]{1,0:T(8,128)}) custom-call(s32[8]{0:T(128)} %get-tuple-element.170.lo, s32[8]{0:T(128)} %get-tuple-element.169.hi, bf16[2048,1152]{1,0:T(8,128)(2,1)} %add_convert_fusion.q_ref.k_ref.v_ref, bf16[2048,1152]{1,0:T(8,128)(2,1)} %add_convert_fusion.q_ref.k_ref.v_ref, ...), custom_call_target="tpu_custom_call" | custom-call | tf_op jit(solution)/shard_map/attend/pallas_call | solution.py:168
  214.4 9.9 %multiply_convert_fusion.1 = (bf16[1024,3072]{1,0:T(8,128)(2,1)}, f32[1024,3072]{1,0:T(8,128)}) fusion(f32[3072]{0:T(1024)S(1)} %reshape.297, bf16[768,3840]{1,0:T(8,128)(2,1)S(1)} %bitcast.432, f32[1024,768]{1,0:T(8,128)S(1)} %get-tuple-element.161, f32[768]{0:T(1024)S(1)} %get-tuple-element.58, f32[768]{0:T(1024)S(1)} %get-tuple-element.59, ...), kind=kOutput, calls=%fused_computation.7 | convolution fusion | flops 4854644736 | bytes 26767360 | tf_op jit(solution)/shard_map/dot_general | solution.py:26
  224.3 8.0 %fusion.88 = (f32[1024]{0:T(1024)S(1)}, f32[1024,768]{1,0:T(8,128)S(1)}) fusion(f32[768]{0:T(1024)S(1)} %get-tuple-element.57, bf16[1024,3072]{1,0:T(8,128)(2,1)} %get-tuple-element.162, bf16[3072,768]{1,0:T(8,128)(2,1)S(1)} %bitcast.438, f32[768]{0:T(1024)S(1)} %get-tuple-element.58, f32[768]{0:T(1024)S(1)} %get-tuple-element.59, ...), kind=kOutput, calls=%fused_computation.324 | convolution fusion | flops 4837342208 | bytes 17323008 | tf_op jit(solution)/shard_map/dot_general | solution.py:26
  238.0 7.1 %convolution_convert_fusion = bf16[3072,768]{1,0:T(8,128)(2,1)} fusion(bf16[1024,3072]{1,0:T(8,128)(2,1)S(1)} %bitcast.480, f32[1024,768]{1,0:T(8,128)S(1)} %get-tuple-element.74), kind=kOutput, calls=%fused_computation.11 | convolution fusion | flops 4834983936 | bytes 14155776 | tf_op jit(solution)/shard_map/dot_general | solution.py:298
  245.1 13.1 %fusion.89 = (bf16[3072]{0:T(1024)(128)(2,1)S(1)}, bf16[1024,3072]{1,0:T(8,128)(2,1)}) fusion(f32[1024,3072]{1,0:T(8,128)} %get-tuple-element.163, f32[3072]{0:T(1024)S(1)} %reshape.297, bf16[3072,768]{1,0:T(8,128)(2,1)S(1)} %bitcast.439, f32[1024,768]{1,0:T(8,128)S(1)} %get-tuple-element.74), kind=kOutput, calls=%fused_computation.325 | convolution fusion | flops 4876661760 | bytes 26757120 | tf_op jit(solution)/shard_map/dot_general | solution.py:302
  258.1 10.1 %convolution_convert_fusion.1 = bf16[768,3072]{1,0:T(8,128)(2,1)} fusion(bf16[1024,3072]{1,0:T(8,128)(2,1)} %get-tuple-element.168, f32[1024,768]{1,0:T(8,128)S(1)} %get-tuple-element.161, f32[768]{0:T(1024)S(1)} %get-tuple-element.58, f32[768]{0:T(1024)S(1)} %get-tuple-element.59, f32[1024]{0:T(1024)S(1)} %add_rsqrt_fusion.1, ...), kind=kOutput, calls=%fused_computation.12 | convolution fusion | flops 4838129664 | bytes 14170112 | tf_op jit(solution)/shard_map/dot_general | solution.py:298
  268.2 9.4 %multiply_reduce_fusion = (bf16[768]{0:T(1024)(128)(2,1)S(1)}, f32[1024]{0:T(1024)S(1)}, f32[1024]{0:T(1024)S(1)}, bf16[768]{0:T(1024)(128)(2,1)S(1)}, f32[1024,768]{1,0:T(8,128)}) fusion(f32[1024,768]{1,0:T(8,128)S(1)} %get-tuple-element.161, f32[1024]{0:T(1024)S(1)} %add_rsqrt_fusion.1, f32[1024]{0:T(1024)S(1)} %broadcast_multiply_fusion.4, ...), kind=kOutput, calls=%fused_computation.40 | convolution fusion | flops 4839698432 | bytes 20470784 | tf_op jit(solution)/shard_map/dot_general | solution.py:302
  310.3 32.1 %attend_back.2 = (bf16[1024,384]{1,0:T(8,128)(2,1)}, f32[2048,384]{1,0:T(8,128)}, f32[2048,384]{1,0:T(8,128)}) custom-call(s32[8]{0:T(128)} %get-tuple-element.170.lo, s32[8]{0:T(128)} %get-tuple-element.169.hi, bf16[2048,1152]{1,0:T(8,128)(2,1)} %add_convert_fusion.q_ref.k_ref.v_ref, bf16[2048,1152]{1,0:T(8,128)(2,1)} %add_convert_fusion.q_ref.k_ref.v_ref, ...), custom_call_target="tpu_custom_call" | custom-call | tf_op jit(solution)/shard_map/attend_back/pallas_call | solution.py:205
  343.6 40.9 %attend_back.3 = (bf16[1024,384]{1,0:T(8,128)(2,1)}, bf16[2048,384]{1,0:T(8,128)(2,1)}, bf16[2048,384]{1,0:T(8,128)(2,1)}) custom-call(s32[8]{0:T(128)} %get-tuple-element.170.lo, s32[8]{0:T(128)} %get-tuple-element.169.hi, bf16[2048,1152]{1,0:T(8,128)(2,1)} %add_convert_fusion.q_ref.k_ref.v_ref, bf16[2048,1152]{1,0:T(8,128)(2,1)} %add_convert_fusion.q_ref.k_ref.v_ref, ...), custom_call_target="tpu_custom_call" | custom-call | tf_op jit(solution)/shard_map/attend_back/pallas_call | solution.py:205
  405.2 7.2 %collective-permute-start.29 = (bf16[2,2,2,48,640]{4,3,2,1,0:T(8,128)(2,1)S(1)}, bf16[2,2,2,48,640]{4,3,2,1,0:T(8,128)(2,1)S(1)}, u32[]{:S(2)}, u32[]{:S(2)}) collective-permute-start(bf16[2,2,2,48,640]{4,3,2,1,0:T(8,128)(2,1)S(1)} %fusion.59), channel_id=1, source_target_pairs={{0,4},{4,0},{8,12},{12,8},{16,20},{20,16},{24,28},{28,24},{1,5},{5... | collective-permute-start | bytes 1474568 | tf_op jit(solution)/shard_map/ppermute | solution.py:242
  416.2 11.0 %collective-permute-done.36 = bf16[2,2,24,896]{3,2,1,0:T(8,128)(2,1)S(1)} collective-permute-done((bf16[2,2,24,896]{3,2,1,0:T(8,128)(2,1)S(1)}, bf16[2,2,24,896]{3,2,1,0:T(8,128)(2,1)S(1)}, u32[]{:S(2)}, u32[]{:S(2)}) %collective-permute-start.36) | collective-permute-done | bytes 172064 | tf_op jit(solution)/shard_map/ppermute | solution.py:242
  491.6 17.7 %collective-permute-done.45 = bf16[2,2,2,96,768]{4,3,0,1,2:T(8,128)(2,1)S(1)} collective-permute-done((bf16[2,2,2,96,768]{4,3,0,1,2:T(8,128)(2,1)S(1)}, bf16[2,2,2,96,768]{4,3,0,1,2:T(8,128)(2,1)S(1)}, u32[]{:S(2)}, u32[]{:S(2)}) %collective-permute-start.45) | collective-permute-done | bytes 1179680 | tf_op jit(solution)/shard_map/ppermute | solution.py:242
  515.2 15.8 %collective-permute-done.24 = bf16[512,768]{1,0:T(8,128)(2,1)S(1)} collective-permute-done((bf16[512,768]{1,0:T(8,128)(2,1)S(1)}, bf16[512,768]{1,0:T(8,128)(2,1)S(1)}, u32[]{:S(2)}, u32[]{:S(2)}) %collective-permute-start.24) | collective-permute-done | bytes 786464 | tf_op jit(solution)/shard_map/ppermute | solution.py:242
  533.1 10.1 %collective-permute-done.46 = bf16[2,2,96,768]{3,2,0,1:T(8,128)(2,1)S(1)} collective-permute-done((bf16[2,2,96,768]{3,2,0,1:T(8,128)(2,1)S(1)}, bf16[2,2,96,768]{3,2,0,1:T(8,128)(2,1)S(1)}, u32[]{:S(2)}, u32[]{:S(2)}) %collective-permute-start.46) | collective-permute-done | bytes 589856 | tf_op jit(solution)/shard_map/ppermute | solution.py:242
  545.8 7.6 %collective-permute-done.47 = bf16[2,96,768]{2,1,0:T(8,128)(2,1)S(1)} collective-permute-done((bf16[2,96,768]{2,1,0:T(8,128)(2,1)S(1)}, bf16[2,96,768]{2,1,0:T(8,128)(2,1)S(1)}, u32[]{:S(2)}, u32[]{:S(2)}) %collective-permute-start.47) | collective-permute-done | bytes 294944 | tf_op jit(solution)/shard_map/ppermute | solution.py:242
  554.2 6.7 %collective-permute-done.42 = bf16[2,24,3072]{2,1,0:T(8,128)(2,1)S(1)} collective-permute-done((bf16[2,24,3072]{2,1,0:T(8,128)(2,1)S(1)}, bf16[2,24,3072]{2,1,0:T(8,128)(2,1)S(1)}, u32[]{:S(2)}, u32[]{:S(2)}) %collective-permute-start.42) | collective-permute-done | bytes 294944 | tf_op jit(solution)/shard_map/ppermute | solution.py:242
  (395 shorter events, 253.0 us)
Async XLA Ops:
  11.6 48.6 %collective-permute-start = (bf16[512,768]{1,0:T(8,128)(2,1)S(1)}, bf16[512,768]{1,0:T(8,128)(2,1)S(1)}, u32[]{:S(2)}, u32[]{:S(2)}) collective-permute-start(bf16[512,768]{1,0:T(8,128)(2,1)S(1)} %dynamic-slice_bitcast_fusion.5), channel_id=1, source_target_pairs={{0,2},{2,0},{1,3},{3,1},{4,6},{6,4},{5,7},{7,5},{8,10},{10,8},{9,1... | collective-permute-start | bytes 2359304 | tf_op jit(solution)/shard_map/ppermute | solution.py:242
  15.4 46.6 %collective-permute-start.21 = (bf16[512,768]{1,0:T(8,128)(2,1)S(1)}, bf16[512,768]{1,0:T(8,128)(2,1)S(1)}, u32[]{:S(2)}, u32[]{:S(2)}) collective-permute-start(bf16[512,768]{1,0:T(8,128)(2,1)S(1)} %dynamic-slice_bitcast_fusion.2), channel_id=1, source_target_pairs={{0,2},{2,0},{1,3},{3,1},{4,6},{6,4},{5,7},{7,5},{8,10},{10,8},{9,1... | collective-permute-start | bytes 2359304 | tf_op jit(solution)/shard_map/ppermute | solution.py:242
  38.9 17.4 %collective-permute-start.5 = (bf16[2,2,48,640]{3,2,0,1:T(8,128)(2,1)S(1)}, bf16[2,2,48,640]{3,2,0,1:T(8,128)(2,1)S(1)}, u32[]{:S(2)}, u32[]{:S(2)}) collective-permute-start(bf16[2,2,48,640]{3,2,0,1:T(8,128)(2,1)S(1)} %get-tuple-element.130), channel_id=1, source_target_pairs={{0,4},{4,0},{8,12},{12,8},{16,20},{20,16},{24,28},{28,24},{1,5},{5... | collective-permute-start | bytes 737288 | tf_op jit(solution)/shard_map/ppermute | solution.py:242
  40.4 17.9 %collective-permute-start.7 = (bf16[2,2,48,640]{3,2,0,1:T(8,128)(2,1)S(1)}, bf16[2,2,48,640]{3,2,0,1:T(8,128)(2,1)S(1)}, u32[]{:S(2)}, u32[]{:S(2)}) collective-permute-start(bf16[2,2,48,640]{3,2,0,1:T(8,128)(2,1)S(1)} %get-tuple-element.131), channel_id=1, source_target_pairs={{0,2},{2,0},{1,3},{3,1},{4,6},{6,4},{5,7},{7,5},{8,10},{10,8},{9,1... | collective-permute-start | bytes 737288 | tf_op jit(solution)/shard_map/ppermute | solution.py:242
  58.5 34.2 %collective-permute-start.6 = (bf16[2,2,2,48,640]{4,3,0,1,2:T(8,128)(2,1)S(1)}, bf16[2,2,2,48,640]{4,3,0,1,2:T(8,128)(2,1)S(1)}, u32[]{:S(2)}, u32[]{:S(2)}) collective-permute-start(bf16[2,2,2,48,640]{4,3,0,1,2:T(8,128)(2,1)S(1)} %pad_maximum_fusion.17), channel_id=1, source_target_pairs={{0,2},{2,0},{1,3},{3,1},{4,6},{6,4},{5,7},{7,5},{8,10},{10,8},{9,1... | collective-permute-start | bytes 1474568 | tf_op jit(solution)/shard_map/ppermute | solution.py:242
  62.0 30.9 %collective-permute-start.1 = (bf16[2,512,768]{2,1,0:T(8,128)(2,1)S(1)}, bf16[2,512,768]{2,1,0:T(8,128)(2,1)S(1)}, u32[]{:S(2)}, u32[]{:S(2)}) collective-permute-start(bf16[2,512,768]{2,1,0:T(8,128)(2,1)S(1)} %pad_maximum_fusion.6), channel_id=1, source_target_pairs={{0,1},{1,0},{2,3},{3,2},{4,5},{5,4},{6,7},{7,6},{8,9},{9,8},{10,11... | collective-permute-start | bytes 4718600 | tf_op jit(solution)/shard_map/ppermute | solution.py:242
  71.4 19.4 %collective-permute-start.12 = (bf16[2,2,24,3840]{3,2,0,1:T(8,128)(2,1)S(1)}, bf16[2,2,24,3840]{3,2,0,1:T(8,128)(2,1)S(1)}, u32[]{:S(2)}, u32[]{:S(2)}) collective-permute-start(bf16[2,2,24,3840]{3,2,0,1:T(8,128)(2,1)S(1)} %pad_maximum_fusion.14), channel_id=1, source_target_pairs={{0,4},{4,0},{8,12},{12,8},{16,20},{20,16},{24,28},{28,24},{1,5},{5... | collective-permute-start | bytes 2211848 | tf_op jit(solution)/shard_map/ppermute | solution.py:242
  82.3 30.3 %collective-permute-start.18 = (bf16[2,2,2,96,768]{4,3,0,1,2:T(8,128)(2,1)S(1)}, bf16[2,2,2,96,768]{4,3,0,1,2:T(8,128)(2,1)S(1)}, u32[]{:S(2)}, u32[]{:S(2)}) collective-permute-start(bf16[2,2,2,96,768]{4,3,0,1,2:T(8,128)(2,1)S(1)} %pad_maximum_fusion.12), channel_id=1, source_target_pairs={{0,4},{4,0},{8,12},{12,8},{16,20},{20,16},{24,28},{28,24},{1,5},{5... | collective-permute-start | bytes 3538952 | tf_op jit(solution)/shard_map/ppermute | solution.py:242
  91.1 27.3 %collective-permute-start.13 = (bf16[2,2,2,24,3840]{4,3,0,1,2:T(8,128)(2,1)S(1)}, bf16[2,2,2,24,3840]{4,3,0,1,2:T(8,128)(2,1)S(1)}, u32[]{:S(2)}, u32[]{:S(2)}) collective-permute-start(bf16[2,2,2,24,3840]{4,3,0,1,2:T(8,128)(2,1)S(1)} %pad_maximum_fusion.11), channel_id=1, source_target_pairs={{0,2},{2,0},{1,3},{3,1},{4,6},{6,4},{5,7},{7,5},{8,10},{10,8},{9,1... | collective-permute-start | bytes 4423688 | tf_op jit(solution)/shard_map/ppermute | solution.py:242
  114.5 88.1 %collective-permute-start.19 = (bf16[2,2,2,2,96,768]{5,4,3,2,1,0:T(8,128)(2,1)}, bf16[2,2,2,2,96,768]{5,4,3,2,1,0:T(8,128)(2,1)}, u32[]{:S(2)}, u32[]{:S(2)}) collective-permute-start(bf16[2,2,2,2,96,768]{5,4,3,2,1,0:T(8,128)(2,1)} %maximum_bitcast_fusion.1), channel_id=1, source_target_pairs={{0,1},{1,0},{2,3},{3,2},{4,5},{5,4},{6,7},{7,6},{8,9},{9,8},{10,11... | collective-permute-start | bytes 7077896 | tf_op jit(solution)/shard_map/ppermute | solution.py:242
  120.8 86.6 %collective-permute-start.14 = (bf16[2,2,2,2,24,3840]{5,4,3,2,1,0:T(8,128)(2,1)}, bf16[2,2,2,2,24,3840]{5,4,3,2,1,0:T(8,128)(2,1)}, u32[]{:S(2)}, u32[]{:S(2)}) collective-permute-start(bf16[2,2,2,2,24,3840]{5,4,3,2,1,0:T(8,128)(2,1)} %maximum_bitcast_fusion), channel_id=1, source_target_pairs={{0,1},{1,0},{2,3},{3,2},{4,5},{5,4},{6,7},{7,6},{8,9},{9,8},{10,11... | collective-permute-start | bytes 8847368 | tf_op jit(solution)/shard_map/ppermute | solution.py:242
  281.0 197.4 %collective-permute-start.44 = (bf16[2,2,2,2,96,768]{5,4,0,1,3,2:T(8,128)(2,1)}, bf16[2,2,2,2,96,768]{5,4,0,1,3,2:T(8,128)(2,1)}, u32[]{:S(2)}, u32[]{:S(2)}) collective-permute-start(bf16[2,2,2,2,96,768]{5,4,0,1,3,2:T(8,128)(2,1)} %bitcast.416), channel_id=1, source_target_pairs={{0,1},{1,0},{2,3},{3,2},{4,5},{5,4},{6,7},{7,6},{8,9},{9,8},{10,11... | collective-permute-start | bytes 7077896 | tf_op jit(solution)/shard_map/ppermute | solution.py:242
  301.3 179.6 %collective-permute-start.39 = (bf16[2,2,2,2,24,3072]{5,4,0,1,2,3:T(8,128)(2,1)}, bf16[2,2,2,2,24,3072]{5,4,0,1,2,3:T(8,128)(2,1)}, u32[]{:S(2)}, u32[]{:S(2)}) collective-permute-start(bf16[2,2,2,2,24,3072]{5,4,0,1,2,3:T(8,128)(2,1)} %bitcast.417), channel_id=1, source_target_pairs={{0,1},{1,0},{2,3},{3,2},{4,5},{5,4},{6,7},{7,6},{8,9},{9,8},{10,11... | collective-permute-start | bytes 7077896 | tf_op jit(solution)/shard_map/ppermute | solution.py:242
  303.5 110.0 %collective-permute-start.20 = (bf16[512,768]{1,0:T(8,128)(2,1)}, bf16[512,768]{1,0:T(8,128)(2,1)}, u32[]{:S(2)}, u32[]{:S(2)}) collective-permute-start(bf16[512,768]{1,0:T(8,128)(2,1)} %dynamic-slice_bitcast_fusion.3), channel_id=1, source_target_pairs={{0,2},{2,0},{1,3},{3,1},{4,6},{6,4},{5,7},{7,5},{8,10},{10,8},{9,1... | collective-permute-start | bytes 2359304 | tf_op jit(solution)/shard_map/ppermute | solution.py:242
  307.1 98.1 %collective-permute-start.35 = (bf16[2,2,2,24,896]{4,3,2,1,0:T(8,128)(2,1)}, bf16[2,2,2,24,896]{4,3,2,1,0:T(8,128)(2,1)}, u32[]{:S(2)}, u32[]{:S(2)}) collective-permute-start(bf16[2,2,2,24,896]{4,3,2,1,0:T(8,128)(2,1)} %dynamic-slice_bitcast_fusion.8), channel_id=1, source_target_pairs={{0,2},{2,0},{1,3},{3,1},{4,6},{6,4},{5,7},{7,5},{8,10},{10,8},{9,1... | collective-permute-start | bytes 1032200 | tf_op jit(solution)/shard_map/ppermute | solution.py:242
  395.5 31.7 %collective-permute-start.25 = (bf16[2,2,2,48,640]{4,3,0,1,2:T(8,128)(2,1)}, bf16[2,2,2,48,640]{4,3,0,1,2:T(8,128)(2,1)}, u32[]{:S(2)}, u32[]{:S(2)}) collective-permute-start(bf16[2,2,2,48,640]{4,3,0,1,2:T(8,128)(2,1)} %bitcast.418), channel_id=1, source_target_pairs={{0,2},{2,0},{1,3},{3,1},{4,6},{6,4},{5,7},{7,5},{8,10},{10,8},{9,1... | collective-permute-start | bytes 1474568 | tf_op jit(solution)/shard_map/ppermute | solution.py:242
  405.2 28.6 %collective-permute-start.29 = (bf16[2,2,2,48,640]{4,3,2,1,0:T(8,128)(2,1)S(1)}, bf16[2,2,2,48,640]{4,3,2,1,0:T(8,128)(2,1)S(1)}, u32[]{:S(2)}, u32[]{:S(2)}) collective-permute-start(bf16[2,2,2,48,640]{4,3,2,1,0:T(8,128)(2,1)S(1)} %fusion.59), channel_id=1, source_target_pairs={{0,4},{4,0},{8,12},{12,8},{16,20},{20,16},{24,28},{28,24},{1,5},{5... | collective-permute-start | bytes 1474568 | tf_op jit(solution)/shard_map/ppermute | solution.py:242
  427.2 59.9 %collective-permute-start.23 = (bf16[1024,768]{1,0:T(8,128)(2,1)}, bf16[1024,768]{1,0:T(8,128)(2,1)}, u32[]{:S(2)}, u32[]{:S(2)}) collective-permute-start(bf16[1024,768]{1,0:T(8,128)(2,1)} %convolution_convert_fusion.2), channel_id=1, source_target_pairs={{0,1},{1,0},{2,3},{3,2},{4,5},{5,4},{6,7},{7,6},{8,9},{9,8},{10,11... | collective-permute-start | bytes 4718600 | tf_op jit(solution)/shard_map/ppermute | solution.py:242
  442.0 28.7 %collective-permute-start.38 = (bf16[24,896]{1,0:T(8,128)(2,1)S(1)}, bf16[24,896]{1,0:T(8,128)(2,1)S(1)}, u32[]{:S(2)}, u32[]{:S(2)}) collective-permute-start(bf16[24,896]{1,0:T(8,128)(2,1)S(1)} %dynamic-slice_bitcast_fusion.23), channel_id=1, source_target_pairs={{0,16},{4,20},{8,24},{12,28},{16,0},{20,4},{24,8},{28,12},{1,17},{... | collective-permute-start | bytes 129032 | tf_op jit(solution)/shard_map/ppermute | solution.py:242
  480.9 28.4 %collective-permute-start.45 = (bf16[2,2,2,96,768]{4,3,0,1,2:T(8,128)(2,1)S(1)}, bf16[2,2,2,96,768]{4,3,0,1,2:T(8,128)(2,1)S(1)}, u32[]{:S(2)}, u32[]{:S(2)}) collective-permute-start(bf16[2,2,2,96,768]{4,3,0,1,2:T(8,128)(2,1)S(1)} %dynamic-slice_bitcast_fusion), channel_id=1, source_target_pairs={{0,4},{4,0},{8,12},{12,8},{16,20},{20,16},{24,28},{28,24},{1,5},{5... | collective-permute-start | bytes 3538952 | tf_op jit(solution)/shard_map/ppermute | solution.py:242
  485.3 28.9 %collective-permute-start.40 = (bf16[2,2,2,24,3072]{4,3,0,1,2:T(8,128)(2,1)S(1)}, bf16[2,2,2,24,3072]{4,3,0,1,2:T(8,128)(2,1)S(1)}, u32[]{:S(2)}, u32[]{:S(2)}) collective-permute-start(bf16[2,2,2,24,3072]{4,3,0,1,2:T(8,128)(2,1)S(1)} %dynamic-slice_bitcast_fusion.1), channel_id=1, source_target_pairs={{0,2},{2,0},{1,3},{3,1},{4,6},{6,4},{5,7},{7,5},{8,10},{10,8},{9,1... | collective-permute-start | bytes 3538952 | tf_op jit(solution)/shard_map/ppermute | solution.py:242
  490.9 40.2 %collective-permute-start.24 = (bf16[512,768]{1,0:T(8,128)(2,1)S(1)}, bf16[512,768]{1,0:T(8,128)(2,1)S(1)}, u32[]{:S(2)}, u32[]{:S(2)}) collective-permute-start(bf16[512,768]{1,0:T(8,128)(2,1)S(1)} %fusion.44), channel_id=1, source_target_pairs={{0,2},{2,0},{1,3},{3,1},{4,6},{6,4},{5,7},{7,5},{8,10},{10,8},{9,1... | collective-permute-start | bytes 2359304 | tf_op jit(solution)/shard_map/ppermute | solution.py:242
  509.7 33.5 %collective-permute-start.46 = (bf16[2,2,96,768]{3,2,0,1:T(8,128)(2,1)S(1)}, bf16[2,2,96,768]{3,2,0,1:T(8,128)(2,1)S(1)}, u32[]{:S(2)}, u32[]{:S(2)}) collective-permute-start(bf16[2,2,96,768]{3,2,0,1:T(8,128)(2,1)S(1)} %dynamic-slice_bitcast_fusion.6), channel_id=1, source_target_pairs={{0,2},{2,0},{1,3},{3,1},{4,6},{6,4},{5,7},{7,5},{8,10},{10,8},{9,1... | collective-permute-start | bytes 1769480 | tf_op jit(solution)/shard_map/ppermute | solution.py:242
  514.6 28.9 %collective-permute-start.41 = (bf16[2,2,24,3072]{3,2,0,1:T(8,128)(2,1)S(1)}, bf16[2,2,24,3072]{3,2,0,1:T(8,128)(2,1)S(1)}, u32[]{:S(2)}, u32[]{:S(2)}) collective-permute-start(bf16[2,2,24,3072]{3,2,0,1:T(8,128)(2,1)S(1)} %dynamic-slice_bitcast_fusion.7), channel_id=1, source_target_pairs={{0,4},{4,0},{8,12},{12,8},{16,20},{20,16},{24,28},{28,24},{1,5},{5... | collective-permute-start | bytes 1769480 | tf_op jit(solution)/shard_map/ppermute | solution.py:242
  (75 other events, 767.1 us)
where the time goes:
time: 578 us; the launch traced here: 570 us
  waiting for transfers between devices  168 us (29%)
  Pallas kernels  126 us (22%)
  matrix products  82.1 us (14%)
  local copies, waits for them, and re-layouts  70.7 us (12%)
  starting transfers between devices  62.7 us (11%)
  other arithmetic  58.3 us (10%)
    ppermute x49, waiting for transfers between devices, swap(): return lax.ppermute(values, axis, [(i, i ^ step) for i in range(count)])  168 us
    pallas_call x2, Pallas kernels, attend_back(): pl.pallas_call(functools.partial(attend_back_kernel, base=base, last=last...  73 us
    ppermute x49, starting transfers between devices, swap(): return lax.ppermute(values, axis, [(i, i ^ step) for i in range(count)])  62.7 us
    pallas_call x3, Pallas kernels, attend(): pl.pallas_call(functools.partial(attend_kernel, base=base), out_shape=(ja...  52.5 us
    dot_general x5, matrix products, dot_cols(): lax.dot_general(left, right, (((1,), (1,)), ((), ())), preferred_element_...  33.4 us
    dot_general x4, matrix products, dot(): return jnp.dot(left, right, preferred_element_type=f32)  25.9 us
    dot_general x4, matrix products, dot_rows(): lax.dot_general(left, right, (((0,), (0,)), ((), ())), preferred_element_...  22.9 us
    another operation x42, other arithmetic, in_order(): return jnp.stack([low, high], axis=dim)  21.9 us
  transfers between devices with their start and end apart: 49, of which 24 were waited for; matrix products, arithmetic and copies ran while one was open for 22% of the time, Pallas kernels for 22%

commit v1 on v0

--- a/solution.py
+++ b/solution.py
@@ -247,9 +247,9 @@
 
 
 def in_order(bit, mine, other, dim=0):
-    low = jnp.where(bit == 0, mine, other)
-    high = jnp.where(bit == 0, other, mine)
-    return jnp.stack([low, high], axis=dim)
+    mine, other = jnp.expand_dims(mine, dim), jnp.expand_dims(other, dim)
+    place = lax.broadcasted_iota(jnp.int32, (1,) * dim + (2,) + (1,) * (mine.ndim - dim - 1), dim)
+    return jnp.where(place == bit, mine, other)
 
 
 def grow(values, names):
@@ -272,8 +272,8 @@
         dim = left.index(name)
         bit = bit_of(name)
         got = swap(pick(values, 1 - bit, dim), name)
+        left.remove(name)
         values = pick(values, bit, dim).astype(f32) + got.astype(f32)
-        left.remove(name)
         if left:
             values = values.astype(bf16)
     return values
@@ -328,12 +328,16 @@
     rank = lax.axis_index("y") // 2
     blocks = (2,) * len(wanted)
 
-    columns = jnp.stack(
-        [query_bias, value_bias, output_bias, first_gain, first_shift, outer_bias, second_gain, second_shift],
-        axis=1,
+    columns = jnp.concatenate(
+        [
+            query_bias, value_bias, output_bias, first_gain, first_shift, outer_bias, second_gain, second_shift,
+            inner_bias,
+        ]
     )
-    columns = jnp.concatenate([columns, inner_bias.reshape(own, chunks)], axis=1)
-    columns = jnp.pad(columns, ((0, 0), (0, PAIR - columns.shape[1])))
+    used = columns.shape[0]
+    lines = -(-used // PAIR)
+    columns = jnp.pad(columns, (0, lines * PAIR - used)).reshape(lines, PAIR)
+    columns = jnp.pad(columns, ((0, own - lines), (0, 0)))
 
     def three(index):
         return jnp.concatenate(
@@ -361,11 +365,12 @@
     part_b = sort_blocks(part_b, far + y_names + [near], wanted).reshape(width, 3 * half + PAIR - cut)
     joined = jnp.concatenate([part_a, part_b], axis=1)
     qkv_weight = joined[:, : 3 * half]
-    vectors = joined[:, 3 * half :].astype(f32).T
+    vectors = joined[:, 3 * half :].reshape(-1, own, PAIR)[:, :lines].reshape(-1, lines * PAIR).astype(f32)
+    inner_bias = vectors[:, 8 * own : used].reshape(hidden)
+    vectors = vectors[:, : 8 * own].reshape(-1, 8, own).transpose(1, 0, 2).reshape(8, width)
     half_of = lambda row: lax.dynamic_slice_in_dim(row, c * half, half, 0)
     qkv_bias = jnp.concatenate([half_of(vectors[0]), jnp.zeros((half,), f32), half_of(vectors[1])])
     output_bias, first_gain, first_shift, outer_bias, second_gain, second_shift = [vectors[k] for k in range(2, 8)]
-    inner_bias = joined[:, 3 * half + 8 : 3 * half + 8 + chunks].reshape(hidden).astype(f32)
 
     output_inner = grow(output_inner, far)
     outer_part = grow(outer_part, far)
@@ -389,10 +394,12 @@
     mixed_all = jnp.concatenate([a[0] for a in attended], axis=0)
     log_sums = jnp.concatenate([a[1] for a in attended], axis=1)
     mixed_heads = pick(mixed_all.reshape(-1, 2, 2, local, half), rank, 0)
-    got = swap(pick(mixed_heads, 1 - c, 1), core)
-    mixed = in_order(c, pick(mixed_heads, c, 1), got, 2).reshape(2 * local, width)
-
-    pre = source.astype(f32) + dot(mixed, output_weight) + output_bias
+    got = swap(pick(mixed_heads, 1 - c, 1), core).reshape(2 * local, half)
+    kept = pick(mixed_heads, c, 1).reshape(2 * local, half)
+    weight_kept = lax.dynamic_slice_in_dim(output_weight, c * half, half, 0)
+    weight_got = lax.dynamic_slice_in_dim(output_weight, (1 - c) * half, half, 0)
+
+    pre = source.astype(f32) + dot(kept, weight_kept) + dot(got, weight_got) + output_bias
     first_unit, first_inverse = norm_stats(pre)
     first = first_unit * first_gain + first_shift
     first_low = first.astype(bf16)
@@ -405,8 +412,8 @@
     result = (second_unit * second_gain + second_shift).astype(bf16).reshape(2, local, width)
 
     def to_owner(values):
-        kept = pick(values, y, 0)
-        return in_order(y, kept, swap(pick(values, 1 - y, 0).astype(bf16), partner).astype(kept.dtype))
+        stays = pick(values, y, 0)
+        return in_order(y, stays, swap(pick(values, 1 - y, 0).astype(bf16), partner).astype(stays.dtype))
 
     layer_output = to_owner(result)
 
@@ -428,14 +435,15 @@
     back = list(reversed(far))
     g_outer_weight = core_then_chips(dot_rows(active, d_outer), [near] + y_names + back)
     d_inner = (dot_cols(d_outer, outer_weight) * slope.astype(f32)).astype(bf16)
-    g_inner_weight = core_then_chips(dot_rows(first_low, d_inner), y_names + [near] + back)
+    g_inner = dot_rows(first_low, d_inner)
+    g_inner_weight = core_then_chips(g_inner, y_names + [near] + back)
     d_first = dot_cols(d_inner, inner_weight) + d_total
     d_pre = norm_back(d_first, first_gain, first_unit, first_inverse)
     d_attended = d_pre.astype(bf16)
-    d_mixed = dot_cols(d_attended, output_weight).astype(bf16)
-    d_mixed = d_mixed.reshape(2 * local, 2, half)
-    got = swap(pick(d_mixed, 1 - c, 1), core)
-    d_heads = in_order(c, pick(d_mixed, c, 1).reshape(2, local, half), got.reshape(2, local, half), 1)
+    back_got = dot_cols(d_attended, weight_got).astype(bf16).reshape(2, local, half)
+    back_got = swap(back_got, core)
+    back_kept = dot_cols(d_attended, weight_kept).astype(bf16).reshape(2, local, half)
+    d_heads = in_order(c, back_kept, back_got, 1)
     d_heads = grow(d_heads, reversed(team)).reshape(length, half)
 
     g_columns = jnp.stack(
@@ -451,9 +459,10 @@
     )
     g_columns = jnp.concatenate([g_columns, column_sums(d_inner).reshape(width, chunks)], axis=1)
     g_columns = jnp.pad(g_columns, ((0, 0), (0, PAIR - g_columns.shape[1])))
-    g_output = core_then_chips(
-        jnp.concatenate([dot_rows(mixed, d_attended), g_columns], axis=1), y_names + [near] + back
-    )
+    g_output = in_order(c, dot_rows(kept, d_attended).astype(bf16), dot_rows(got, d_attended).astype(bf16))
+    g_output = g_output.reshape(width, width)
+    g_columns = g_columns.astype(bf16)
+    g_output = core_then_chips(jnp.concatenate([g_output, g_columns], axis=1), y_names + [near] + back)
 
     part = attend_back(qkv, 0, steps // 2, (), mixed_all, d_heads, log_sums, seg_row, seg_col, lo, hi)
     rest = attend_back(
@@ -472,10 +481,10 @@
     g_a = shrink(g_qkv[..., :cut], y_names + [near] + back, wanted)
     g_b = shrink(g_qkv[..., cut:], [near] + y_names + back, wanted)
     g_chip = jnp.concatenate([g_a, g_b], axis=1).reshape(2, own, 3 * half + PAIR)
-    kept = pick(g_chip, c, 0)
-    got = swap(pick(g_chip, 1 - c, 0), core)
-    g_weights = in_order(c, kept[:, : 3 * half], got[:, : 3 * half])
-    g_biases = kept[:, 3 * half :] + got[:, 3 * half :]
+    chip_kept = pick(g_chip, c, 0)
+    chip_got = swap(pick(g_chip, 1 - c, 0), core)
+    g_weights = in_order(c, chip_kept[:, : 3 * half], chip_got[:, : 3 * half])
+    g_biases = chip_kept[:, 3 * half :] + chip_got[:, 3 * half :]
     g_three = [
         jnp.concatenate([g_weights[0, :, k * half : (k + 1) * half], g_weights[1, :, k * half : (k + 1) * half]], axis=1)
         for k in range(3)

time: 578 us -> 598 us (1.035)
  waiting for transfers between devices: 168 us -> 126 us
  other arithmetic: 58.3 us -> 90 us
  local copies, waits for them, and re-layouts: 70.7 us -> 94.9 us
    select_n x1 -> x29, other arithmetic: 1.29 us -> 52.1 us  [in_order(): return jnp.where(place == bit, mine, other)]
    ppermute x49, waiting for transfers between devices: 168 us -> 126 us  [swap(): return lax.ppermute(values, axis, [(i, i ^ step) for i in range(count)])]
    broadcast_in_dim x0 -> x23, local copies, waits for them, and re-layouts: none -> 34.2 us  [in_order(): return jnp.where(place == bit, mine, other)]
    another operation x42 -> x0, other arithmetic: 21.9 us -> none  [in_order(): return jnp.stack([low, high], axis=dim)]
    unnamed x111 -> x151, local copies, waits for them, and re-layouts: 17.4 us -> 8.3 us
    another operation x9 -> x0, local copies, waits for them, and re-layouts: 7.59 us -> none  [the longest x8 5.97 us: on_device(): jnp.stack([query_bias, value_bias, output_bias, first_gain, first_shift,...]
    dot_general x2 -> x0, local copies, waits for them, and re-layouts: 7.38 us -> none  [dot_rows(): lax.dot_general(left, right, (((0,), (0,)), ((), ())), preferred_element_...]
    concatenate x1, local copies, waits for them, and re-layouts: 0.11 us -> 6.1 us  [on_device(): jnp.concatenate([query_bias, value_bias, output_bias, first_gain, first_s...]
  transfers between devices with their start and end apart: 49 -> 49, of which waited for: 24 -> 24; matrix products, arithmetic and copies ran while one was open for 22% -> 30% of each run, Pallas kernels for 22% -> 21%
where the time goes in v1:
time: 598 us; the launch traced here: 593 us
  waiting for transfers between devices  126 us (21%)
  Pallas kernels  126 us (21%)
  local copies, waits for them, and re-layouts  94.9 us (16%)
  other arithmetic  90 us (15%)
  matrix products  85.8 us (14%)
  starting transfers between devices  67.8 us (11%)
    ppermute x49, waiting for transfers between devices, swap(): return lax.ppermute(values, axis, [(i, i ^ step) for i in range(count)])  126 us
    pallas_call x2, Pallas kernels, attend_back(): pl.pallas_call(functools.partial(attend_back_kernel, base=base, last=last...  73.2 us
    ppermute x49, starting transfers between devices, swap(): return lax.ppermute(values, axis, [(i, i ^ step) for i in range(count)])  67.8 us
    pallas_call x3, Pallas kernels, attend(): pl.pallas_call(functools.partial(attend_kernel, base=base), out_shape=(ja...  52.6 us
    select_n x29, other arithmetic, in_order(): return jnp.where(place == bit, mine, other)  52.1 us
    broadcast_in_dim x23, local copies, waits for them, and re-layouts, in_order(): return jnp.where(place == bit, mine, other)  34.2 us
    dot_general x6, matrix products, dot_cols(): lax.dot_general(left, right, (((1,), (1,)), ((), ())), preferred_element_...  32 us
    dot_general x5, matrix products, dot(): return jnp.dot(left, right, preferred_element_type=f32)  27.7 us
  transfers between devices with their start and end apart: 49, of which 24 were waited for; matrix products, arithmetic and copies ran while one was open for 30% of the time, Pallas kernels for 21%

profile of v1, /device:TPU:0, one launch (start us, length us, event | category | flops | bytes accessed | tf_op | source)
XLA Modules:
  0.0 592.9 jit_solution(18147293347114060758)
XLA Ops:
  0.7 6.1 %concatenate.60 = bf16[288]{0:T(512)(128)(2,1)S(1)} concatenate(bf16[24]{0:T(256)(128)(2,1)} %param.22, bf16[24]{0:T(256)(128)(2,1)} %param.25, bf16[24]{0:T(256)(128)(2,1)} %param.27, bf16[24]{0:T(256)(128)(2,1)} %param.28, bf16[24]{0:T(256)(128)(2,1)} %param.29, bf16[24]{0:T(256)(128)(2,1)} %param.33, bf16[24]{0:T(256)(128)(2,1)} %param.34, bf16[24]{0:T(256)(128)(2,1)} %param.35, ...), dimensions={0} | concatenate | bytes 1152 | tf_op jit(solution)/shard_map/concatenate | solution.py:331
  50.4 9.0 %collective-permute-done.9 = bf16[24,3840]{1,0:T(8,128)(2,1)S(1)} collective-permute-done((bf16[24,3840]{1,0:T(8,128)(2,1)}, bf16[24,3840]{1,0:T(8,128)(2,1)S(1)}, u32[]{:S(2)}, u32[]{:S(2)}) %collective-permute-start.9) | collective-permute-done | bytes 184352 | tf_op jit(solution)/shard_map/ppermute | solution.py:242
  80.7 6.1 %broadcast_in_dim.779 = bf16[2048,768]{0,1:T(8,128)(2,1)} reshape(bf16[2,2,512,768]{2,1,0,3:T(2,128)(2,1)} %broadcast_in_dim.778) | data formatting | bytes 6291456 | tf_op jit(solution)/shard_map/jit(_where)/broadcast_in_dim | solution.py:252
  107.7 6.5 %collective-permute-done.11 = bf16[2,2,24,3840]{3,2,0,1:T(8,128)(2,1)S(1)} collective-permute-done((bf16[2,2,24,3840]{3,2,0,1:T(8,128)(2,1)}, bf16[2,2,24,3840]{3,2,0,1:T(8,128)(2,1)S(1)}, u32[]{:S(2)}, u32[]{:S(2)}) %collective-permute-start.11) | collective-permute-done | bytes 737312 | tf_op jit(solution)/shard_map/ppermute | solution.py:242
  135.2 6.1 %broadcast_in_dim.781 = bf16[2048,768]{0,1:T(8,128)(2,1)} reshape(bf16[2,2,512,768]{2,1,0,3:T(2,128)(2,1)} %broadcast_in_dim.780) | data formatting | bytes 6291456 | tf_op jit(solution)/shard_map/jit(_where)/broadcast_in_dim | solution.py:252
  141.4 9.4 %collective-permute-done.12 = bf16[2,2,2,24,3840]{4,3,0,1,2:T(8,128)(2,1)} collective-permute-done((bf16[2,2,2,24,3840]{4,3,0,1,2:T(8,128)(2,1)}, bf16[2,2,2,24,3840]{4,3,0,1,2:T(8,128)(2,1)}, u32[]{:S(2)}, u32[]{:S(2)}) %collective-permute-start.12) | collective-permute-done | bytes 1474592 | tf_op jit(solution)/shard_map/ppermute | solution.py:242
  159.2 6.5 %add_convert_fusion.q_ref.k_ref.v_ref = bf16[2048,1152]{1,0:T(8,128)(2,1)} fusion(bf16[2048,768]{0,1:T(8,128)(2,1)S(1)} %broadcast_select_fusion, f32[1152]{0:T(1024)S(1)} %copy-done.62, bf16[768,640]{1,0:T(8,128)(2,1)S(1)} %copy-done.30, bf16[768,640]{1,0:T(8,128)(2,1)S(1)} %copy-done.32), kind=kOutput, calls=%fused_computation.9 | convolution fusion | flops 3632136192 | bytes 9835008 | tf_op jit(solution)/shard_map/dot_general | solution.py:26
  167.7 17.7 %attend.3 = (bf16[768,384]{1,0:T(8,128)(2,1)}, f32[48,768]{1,0:T(8,128)}) custom-call(s32[8]{0:T(128)} %get-tuple-element.129.lo, s32[8]{0:T(128)} %get-tuple-element.128.hi, bf16[2048,1152]{1,0:T(8,128)(2,1)} %add_convert_fusion.q_ref.k_ref.v_ref, bf16[2048,1152]{1,0:T(8,128)(2,1)} %add_convert_fusion.q_ref.k_ref.v_ref, ...), custom_call_target="tpu_custom_call" | custom-call | tf_op jit(solution)/shard_map/attend/pallas_call | solution.py:168
  185.3 19.9 %attend.4 = (bf16[768,384]{1,0:T(8,128)(2,1)}, f32[48,768]{1,0:T(8,128)}) custom-call(s32[8]{0:T(128)} %get-tuple-element.129.lo, s32[8]{0:T(128)} %get-tuple-element.128.hi, bf16[2048,1152]{1,0:T(8,128)(2,1)} %add_convert_fusion.q_ref.k_ref.v_ref, bf16[2048,1152]{1,0:T(8,128)(2,1)} %add_convert_fusion.q_ref.k_ref.v_ref, ...), custom_call_target="tpu_custom_call" | custom-call | tf_op jit(solution)/shard_map/attend/pallas_call | solution.py:168
  205.2 15.1 %attend.5 = (bf16[512,384]{1,0:T(8,128)(2,1)}, f32[48,512]{1,0:T(8,128)}) custom-call(s32[8]{0:T(128)} %get-tuple-element.129.lo, s32[8]{0:T(128)} %get-tuple-element.128.hi, bf16[2048,1152]{1,0:T(8,128)(2,1)} %add_convert_fusion.q_ref.k_ref.v_ref, bf16[2048,1152]{1,0:T(8,128)(2,1)} %add_convert_fusion.q_ref.k_ref.v_ref, ...), custom_call_target="tpu_custom_call" | custom-call | tf_op jit(solution)/shard_map/attend/pallas_call | solution.py:168
  236.7 9.8 %multiply_convert_fusion.1 = (bf16[1024,3072]{1,0:T(8,128)(2,1)}, f32[1024,3072]{1,0:T(8,128)}) fusion(f32[3072]{0:T(1024)S(1)} %copy-done.59, bf16[768,3840]{1,0:T(8,128)(2,1)S(1)} %bitcast_select_fusion, f32[1024,768]{1,0:T(8,128)S(1)} %get-tuple-element.79, f32[768]{0:T(1024)S(1)} %copy-done.67, f32[768]{0:T(1024)S(1)} %copy-done.51, ...), kind=kOutput, calls=%fused_computation.7 | convolution fusion | flops 4854644736 | bytes 26767360 | tf_op jit(solution)/shard_map/dot_general | solution.py:26
  246.5 7.8 %fusion.75 = (f32[1024]{0:T(1024)S(1)}, f32[1024,768]{1,0:T(8,128)S(1)}) fusion(f32[768]{0:T(1024)S(1)} %copy-done.68, bf16[1024,3072]{1,0:T(8,128)(2,1)} %get-tuple-element.121, bf16[3072,768]{1,0:T(8,128)(2,1)S(1)} %bitcast.293, f32[768]{0:T(1024)S(1)} %copy-done.67, f32[768]{0:T(1024)S(1)} %copy-done.51, f32[1024]{0:T(1024)S(1)} %add_rsqrt_fusion.1, ...), kind=kOutput, calls=%fused_computation.285 | convolution fusion | flops 4837342208 | bytes 17323008 | tf_op jit(solution)/shard_map/dot_general | solution.py:26
  260.3 9.7 %convolution_convert_fusion = bf16[3072,768]{1,0:T(8,128)(2,1)S(1)} fusion(bf16[1024,3072]{1,0:T(8,128)(2,1)} %get-tuple-element.121, f32[1024,768]{1,0:T(8,128)S(1)} %get-tuple-element.74), kind=kOutput, calls=%fused_computation.11 | convolution fusion | flops 4834983936 | bytes 14155776 | tf_op jit(solution)/shard_map/dot_general | solution.py:298
  270.0 13.7 %fusion.76 = (bf16[3072]{0:T(1024)(128)(2,1)}, bf16[1024,3072]{1,0:T(8,128)(2,1)}) fusion(f32[1024,3072]{1,0:T(8,128)} %get-tuple-element.122, f32[3072]{0:T(1024)S(1)} %copy-done.59, bf16[3072,768]{1,0:T(8,128)(2,1)S(1)} %bitcast.293, f32[1024,768]{1,0:T(8,128)S(1)} %get-tuple-element.74), kind=kOutput, calls=%fused_computation.286 | convolution fusion | flops 4876661760 | bytes 26757120 | tf_op jit(solution)/shard_map/dot_general | solution.py:302
  283.8 8.5 %convolution_convert_fusion.1 = bf16[768,3072]{1,0:T(8,128)(2,1)S(1)} fusion(bf16[1024,3072]{1,0:T(8,128)(2,1)} %get-tuple-element.127, f32[1024,768]{1,0:T(8,128)S(1)} %get-tuple-element.79, f32[768]{0:T(1024)S(1)} %copy-done.67, f32[768]{0:T(1024)S(1)} %copy-done.51, f32[1024]{0:T(1024)S(1)} %add_rsqrt_fusion.1, f32[1024]{0:T(1024)S(1)} %broadcast_multiply_fusion.4), kind=kOutput, calls=%fused_computation.12 | convolution fusion | flops 4838129664 | bytes 14170112 | tf_op jit(solution)/shard_map/dot_general | solution.py:298
  292.3 10.0 %multiply_reduce_fusion = (bf16[768]{0:T(1024)(128)(2,1)S(1)}, f32[1024]{0:T(1024)S(1)}, f32[1024]{0:T(1024)S(1)}, bf16[768]{0:T(1024)(128)(2,1)S(1)}, f32[1024,768]{1,0:T(8,128)}) fusion(f32[1024,768]{1,0:T(8,128)S(1)} %get-tuple-element.79, f32[1024]{0:T(1024)S(1)} %add_rsqrt_fusion.1, f32[1024]{0:T(1024)S(1)} %broadcast_multiply_fusion.4, ...), kind=kOutput, calls=%fused_computation.34 | convolution fusion | flops 4839698432 | bytes 20470784 | tf_op jit(solution)/shard_map/dot_general | solution.py:302
  329.7 13.2 %collective-permute-done.20 = bf16[512,768]{1,0:T(8,128)(2,1)S(1)} collective-permute-done((bf16[512,768]{1,0:T(8,128)(2,1)S(1)}, bf16[512,768]{1,0:T(8,128)(2,1)S(1)}, u32[]{:S(2)}, u32[]{:S(2)}) %collective-permute-start.20) | collective-permute-done | bytes 786464 | tf_op jit(solution)/shard_map/ppermute | solution.py:242
  350.1 32.3 %attend_back.2 = (bf16[1024,384]{1,0:T(8,128)(2,1)}, f32[2048,384]{1,0:T(8,128)}, f32[2048,384]{1,0:T(8,128)}) custom-call(s32[8]{0:T(128)} %get-tuple-element.129.lo, s32[8]{0:T(128)} %get-tuple-element.128.hi, bf16[2048,1152]{1,0:T(8,128)(2,1)} %add_convert_fusion.q_ref.k_ref.v_ref, bf16[2048,1152]{1,0:T(8,128)(2,1)} %add_convert_fusion.q_ref.k_ref.v_ref, ...), custom_call_target="tpu_custom_call" | custom-call | tf_op jit(solution)/shard_map/attend_back/pallas_call | solution.py:205
  383.6 40.9 %attend_back.3 = (bf16[1024,384]{1,0:T(8,128)(2,1)}, bf16[2048,384]{1,0:T(8,128)(2,1)}, bf16[2048,384]{1,0:T(8,128)(2,1)}) custom-call(s32[8]{0:T(128)} %get-tuple-element.129.lo, s32[8]{0:T(128)} %get-tuple-element.128.hi, bf16[2048,1152]{1,0:T(8,128)(2,1)} %add_convert_fusion.q_ref.k_ref.v_ref, bf16[2048,1152]{1,0:T(8,128)(2,1)} %add_convert_fusion.q_ref.k_ref.v_ref, ...), custom_call_target="tpu_custom_call" | custom-call | tf_op jit(solution)/shard_map/attend_back/pallas_call | solution.py:205
  437.4 6.3 %collective-permute-start.29 = (bf16[2,2,2,48,640]{4,3,2,1,0:T(8,128)(2,1)S(1)}, bf16[2,2,2,48,640]{4,3,2,1,0:T(8,128)(2,1)S(1)}, u32[]{:S(2)}, u32[]{:S(2)}) collective-permute-start(bf16[2,2,2,48,640]{4,3,2,1,0:T(8,128)(2,1)S(1)} %fusion.48), channel_id=1, source_target_pairs={{0,4},{4,0},{8,12},{12,8},{16,20},{20,16},{24,28},{28,24},{1,5},{5... | collective-permute-start | bytes 1474568 | tf_op jit(solution)/shard_map/ppermute | solution.py:242
  465.2 5.8 collective-permute-start.27
  522.1 29.3 %collective-permute-done.24 = bf16[512,768]{1,0:T(8,128)(2,1)} collective-permute-done((bf16[512,768]{1,0:T(8,128)(2,1)S(1)}, bf16[512,768]{1,0:T(8,128)(2,1)}, u32[]{:S(2)}, u32[]{:S(2)}) %collective-permute-start.24) | collective-permute-done | bytes 786464 | tf_op jit(solution)/shard_map/ppermute | solution.py:242
  560.6 7.2 %collective-permute-done.46 = bf16[2,2,96,768]{3,2,0,1:T(8,128)(2,1)S(1)} collective-permute-done((bf16[2,2,96,768]{3,2,0,1:T(8,128)(2,1)S(1)}, bf16[2,2,96,768]{3,2,0,1:T(8,128)(2,1)S(1)}, u32[]{:S(2)}, u32[]{:S(2)}) %collective-permute-start.46) | collective-permute-done | bytes 589856 | tf_op jit(solution)/shard_map/ppermute | solution.py:242
  571.0 8.1 %collective-permute-done.47 = bf16[2,96,768]{2,1,0:T(8,128)(2,1)S(1)} collective-permute-done((bf16[2,96,768]{2,1,0:T(8,128)(2,1)S(1)}, bf16[2,96,768]{2,1,0:T(8,128)(2,1)S(1)}, u32[]{:S(2)}, u32[]{:S(2)}) %collective-permute-start.47) | collective-permute-done | bytes 294944 | tf_op jit(solution)/shard_map/ppermute | solution.py:242
  (443 shorter events, 285.5 us)
Async XLA Ops:
  11.4 56.0 %collective-permute-start = (bf16[512,768]{1,0:T(8,128)(2,1)}, bf16[512,768]{1,0:T(8,128)(2,1)S(1)}, u32[]{:S(2)}, u32[]{:S(2)}) collective-permute-start(bf16[512,768]{1,0:T(8,128)(2,1)} %get-tuple-element.96), channel_id=1, source_target_pairs={{0,2},{2,0},{1,3},{3,1},{4,6},{6,4},{5,7},{7,5},{8,10},{10,8},{9,1... | collective-permute-start | bytes 2359304 | tf_op jit(solution)/shard_map/ppermute | solution.py:242
  15.0 91.3 %collective-permute-start.21 = (bf16[512,768]{1,0:T(8,128)(2,1)}, bf16[512,768]{1,0:T(8,128)(2,1)S(1)}, u32[]{:S(2)}, u32[]{:S(2)}) collective-permute-start(bf16[512,768]{1,0:T(8,128)(2,1)} %get-tuple-element.90), channel_id=1, source_target_pairs={{0,2},{2,0},{1,3},{3,1},{4,6},{6,4},{5,7},{7,5},{8,10},{10,8},{9,1... | collective-permute-start | bytes 2359304 | tf_op jit(solution)/shard_map/ppermute | solution.py:242
  43.5 20.6 %collective-permute-start.7 = (bf16[2,2,48,640]{3,2,0,1:T(8,128)(2,1)S(1)}, bf16[2,2,48,640]{3,2,0,1:T(8,128)(2,1)S(1)}, u32[]{:S(2)}, u32[]{:S(2)}) collective-permute-start(bf16[2,2,48,640]{3,2,0,1:T(8,128)(2,1)S(1)} %get-tuple-element.101), channel_id=1, source_target_pairs={{0,2},{2,0},{1,3},{3,1},{4,6},{6,4},{5,7},{7,5},{8,10},{10,8},{9,1... | collective-permute-start | bytes 737288 | tf_op jit(solution)/shard_map/ppermute | solution.py:242
  59.4 27.5 %collective-permute-start.16 = (bf16[2,96,768]{2,1,0:T(8,128)(2,1)}, bf16[2,96,768]{2,1,0:T(8,128)(2,1)}, u32[]{:S(2)}, u32[]{:S(2)}) collective-permute-start(bf16[2,96,768]{2,1,0:T(8,128)(2,1)} %broadcast_select_fusion.21), channel_id=1, source_target_pairs={{0,8},{4,12},{8,0},{12,4},{16,24},{20,28},{24,16},{28,20},{1,9},{5... | collective-permute-start | bytes 884744 | tf_op jit(solution)/shard_map/ppermute | solution.py:242
  60.2 30.8 %collective-permute-start.10 = (bf16[2,24,3840]{2,1,0:T(8,128)(2,1)S(1)}, bf16[2,24,3840]{2,1,0:T(8,128)(2,1)}, u32[]{:S(2)}, u32[]{:S(2)}) collective-permute-start(bf16[2,24,3840]{2,1,0:T(8,128)(2,1)S(1)} %broadcast_select_fusion.20), channel_id=1, source_target_pairs={{0,8},{4,12},{8,0},{12,4},{16,24},{20,28},{24,16},{28,20},{1,9},{5... | collective-permute-start | bytes 1105928 | tf_op jit(solution)/shard_map/ppermute | solution.py:242
  64.1 39.2 %collective-permute-start.6 = (bf16[2,2,2,48,640]{4,3,0,1,2:T(8,128)(2,1)}, bf16[2,2,2,48,640]{4,3,0,1,2:T(8,128)(2,1)}, u32[]{:S(2)}, u32[]{:S(2)}) collective-permute-start(bf16[2,2,2,48,640]{4,3,0,1,2:T(8,128)(2,1)} %broadcast_select_fusion.17), channel_id=1, source_target_pairs={{0,2},{2,0},{1,3},{3,1},{4,6},{6,4},{5,7},{7,5},{8,10},{10,8},{9,1... | collective-permute-start | bytes 1474568 | tf_op jit(solution)/shard_map/ppermute | solution.py:242
  67.4 28.0 %collective-permute-start.8 = (bf16[2,2,2,48,640]{4,3,0,1,2:T(8,128)(2,1)}, bf16[2,2,2,48,640]{4,3,0,1,2:T(8,128)(2,1)}, u32[]{:S(2)}, u32[]{:S(2)}) collective-permute-start(bf16[2,2,2,48,640]{4,3,0,1,2:T(8,128)(2,1)} %broadcast_select_fusion.15), channel_id=1, source_target_pairs={{0,4},{4,0},{8,12},{12,8},{16,20},{20,16},{24,28},{28,24},{1,5},{5... | collective-permute-start | bytes 1474568 | tf_op jit(solution)/shard_map/ppermute | solution.py:242
  86.9 38.2 %collective-permute-start.1 = (bf16[2,512,768]{2,1,0:T(8,128)(2,1)}, bf16[2,512,768]{2,1,0:T(8,128)(2,1)}, u32[]{:S(2)}, u32[]{:S(2)}) collective-permute-start(bf16[2,512,768]{2,1,0:T(8,128)(2,1)} %broadcast_select_fusion.5), channel_id=1, source_target_pairs={{0,1},{1,0},{2,3},{3,2},{4,5},{5,4},{6,7},{7,6},{8,9},{9,8},{10,11... | collective-permute-start | bytes 4718600 | tf_op jit(solution)/shard_map/ppermute | solution.py:242
  91.0 27.5 %collective-permute-start.17 = (bf16[2,2,96,768]{3,2,0,1:T(8,128)(2,1)}, bf16[2,2,96,768]{3,2,0,1:T(8,128)(2,1)}, u32[]{:S(2)}, u32[]{:S(2)}) collective-permute-start(bf16[2,2,96,768]{3,2,0,1:T(8,128)(2,1)} %broadcast_select_fusion.13), channel_id=1, source_target_pairs={{0,2},{2,0},{1,3},{3,1},{4,6},{6,4},{5,7},{7,5},{8,10},{10,8},{9,1... | collective-permute-start | bytes 1769480 | tf_op jit(solution)/shard_map/ppermute | solution.py:242
  95.5 18.8 %collective-permute-start.11 = (bf16[2,2,24,3840]{3,2,0,1:T(8,128)(2,1)}, bf16[2,2,24,3840]{3,2,0,1:T(8,128)(2,1)S(1)}, u32[]{:S(2)}, u32[]{:S(2)}) collective-permute-start(bf16[2,2,24,3840]{3,2,0,1:T(8,128)(2,1)} %broadcast_select_fusion.11), channel_id=1, source_target_pairs={{0,4},{4,0},{8,12},{12,8},{16,20},{20,16},{24,28},{28,24},{1,5},{5... | collective-permute-start | bytes 2211848 | tf_op jit(solution)/shard_map/ppermute | solution.py:242
  116.9 33.8 %collective-permute-start.12 = (bf16[2,2,2,24,3840]{4,3,0,1,2:T(8,128)(2,1)}, bf16[2,2,2,24,3840]{4,3,0,1,2:T(8,128)(2,1)}, u32[]{:S(2)}, u32[]{:S(2)}) collective-permute-start(bf16[2,2,2,24,3840]{4,3,0,1,2:T(8,128)(2,1)} %broadcast_select_fusion.6), channel_id=1, source_target_pairs={{0,2},{2,0},{1,3},{3,1},{4,6},{6,4},{5,7},{7,5},{8,10},{10,8},{9,1... | collective-permute-start | bytes 4423688 | tf_op jit(solution)/shard_map/ppermute | solution.py:242
  120.9 33.7 %collective-permute-start.18 = (bf16[2,2,2,96,768]{4,3,0,1,2:T(8,128)(2,1)}, bf16[2,2,2,96,768]{4,3,0,1,2:T(8,128)(2,1)}, u32[]{:S(2)}, u32[]{:S(2)}) collective-permute-start(bf16[2,2,2,96,768]{4,3,0,1,2:T(8,128)(2,1)} %broadcast_select_fusion.9), channel_id=1, source_target_pairs={{0,4},{4,0},{8,12},{12,8},{16,20},{20,16},{24,28},{28,24},{1,5},{5... | collective-permute-start | bytes 3538952 | tf_op jit(solution)/shard_map/ppermute | solution.py:242
  154.6 73.9 %collective-permute-start.13 = (bf16[2,2,2,2,24,3840]{5,4,3,2,1,0:T(8,128)(2,1)}, bf16[2,2,2,2,24,3840]{5,4,3,2,1,0:T(8,128)(2,1)}, u32[]{:S(2)}, u32[]{:S(2)}) collective-permute-start(bf16[2,2,2,2,24,3840]{5,4,3,2,1,0:T(8,128)(2,1)} %broadcast_select_fusion.1), channel_id=1, source_target_pairs={{0,1},{1,0},{2,3},{3,2},{4,5},{5,4},{6,7},{7,6},{8,9},{9,8},{10,11... | collective-permute-start | bytes 8847368 | tf_op jit(solution)/shard_map/ppermute | solution.py:242
  157.7 65.6 %collective-permute-start.19 = (bf16[2,2,2,2,96,768]{5,4,3,2,1,0:T(8,128)(2,1)}, bf16[2,2,2,2,96,768]{5,4,3,2,1,0:T(8,128)(2,1)}, u32[]{:S(2)}, u32[]{:S(2)}) collective-permute-start(bf16[2,2,2,2,96,768]{5,4,3,2,1,0:T(8,128)(2,1)} %broadcast_select_fusion.2), channel_id=1, source_target_pairs={{0,1},{1,0},{2,3},{3,2},{4,5},{5,4},{6,7},{7,6},{8,9},{9,8},{10,11... | collective-permute-start | bytes 7077896 | tf_op jit(solution)/shard_map/ppermute | solution.py:242
  314.1 184.2 %collective-permute-start.44 = (bf16[2,2,2,2,96,768]{5,4,0,1,3,2:T(8,128)(2,1)}, bf16[2,2,2,2,96,768]{5,4,0,1,3,2:T(8,128)(2,1)}, u32[]{:S(2)}, u32[]{:S(2)}) collective-permute-start(bf16[2,2,2,2,96,768]{5,4,0,1,3,2:T(8,128)(2,1)} %bitcast.281), channel_id=1, source_target_pairs={{0,1},{1,0},{2,3},{3,2},{4,5},{5,4},{6,7},{7,6},{8,9},{9,8},{10,11... | collective-permute-start | bytes 7077896 | tf_op jit(solution)/shard_map/ppermute | solution.py:242
  317.6 185.8 %collective-permute-start.39 = (bf16[2,2,2,2,24,3072]{5,4,0,1,2,3:T(8,128)(2,1)}, bf16[2,2,2,2,24,3072]{5,4,0,1,2,3:T(8,128)(2,1)}, u32[]{:S(2)}, u32[]{:S(2)}) collective-permute-start(bf16[2,2,2,2,24,3072]{5,4,0,1,2,3:T(8,128)(2,1)} %bitcast.282), channel_id=1, source_target_pairs={{0,1},{1,0},{2,3},{3,2},{4,5},{5,4},{6,7},{7,6},{8,9},{9,8},{10,11... | collective-permute-start | bytes 7077896 | tf_op jit(solution)/shard_map/ppermute | solution.py:242
  323.3 19.7 %collective-permute-start.20 = (bf16[512,768]{1,0:T(8,128)(2,1)S(1)}, bf16[512,768]{1,0:T(8,128)(2,1)S(1)}, u32[]{:S(2)}, u32[]{:S(2)}) collective-permute-start(bf16[512,768]{1,0:T(8,128)(2,1)S(1)} %get-tuple-element.92), channel_id=1, source_target_pairs={{0,2},{2,0},{1,3},{3,1},{4,6},{6,4},{5,7},{7,5},{8,10},{10,8},{9,1... | collective-permute-start | bytes 2359304 | tf_op jit(solution)/shard_map/ppermute | solution.py:242
  325.7 21.9 %collective-permute-start.22 = (bf16[2,512,384]{2,1,0:T(8,128)(2,1)}, bf16[2,512,384]{2,1,0:T(8,128)(2,1)}, u32[]{:S(2)}, u32[]{:S(2)}) collective-permute-start(bf16[2,512,384]{2,1,0:T(8,128)(2,1)} %bitcast.41), channel_id=1, source_target_pairs={{0,1},{1,0},{2,3},{3,2},{4,5},{5,4},{6,7},{7,6},{8,9},{9,8},{10,11... | collective-permute-start | bytes 2359304 | tf_op jit(solution)/shard_map/ppermute | solution.py:242
  347.7 109.5 %collective-permute-start.34 = (bf16[2,2,2,2,24,896]{5,4,0,1,2,3:T(8,128)(2,1)}, bf16[2,2,2,2,24,896]{5,4,0,1,2,3:T(8,128)(2,1)}, u32[]{:S(2)}, u32[]{:S(2)}) collective-permute-start(bf16[2,2,2,2,24,896]{5,4,0,1,2,3:T(8,128)(2,1)} %fusion.35), channel_id=1, source_target_pairs={{0,1},{1,0},{2,3},{3,2},{4,5},{5,4},{6,7},{7,6},{8,9},{9,8},{10,11... | collective-permute-start | bytes 2064392 | tf_op jit(solution)/shard_map/ppermute | solution.py:242
  449.4 58.7 %collective-permute-start.23 = (bf16[1024,768]{1,0:T(8,128)(2,1)S(1)}, bf16[1024,768]{1,0:T(8,128)(2,1)S(1)}, u32[]{:S(2)}, u32[]{:S(2)}) collective-permute-start(bf16[1024,768]{1,0:T(8,128)(2,1)S(1)} %convolution_convert_fusion.2), channel_id=1, source_target_pairs={{0,1},{1,0},{2,3},{3,2},{4,5},{5,4},{6,7},{7,6},{8,9},{9,8},{10,11... | collective-permute-start | bytes 4718600 | tf_op jit(solution)/shard_map/ppermute | solution.py:242
  463.3 25.8 %collective-permute-start.35 = (bf16[2,2,2,24,896]{4,3,0,1,2:T(8,128)(2,1)S(1)}, bf16[2,2,2,24,896]{4,3,0,1,2:T(8,128)(2,1)S(1)}, u32[]{:S(2)}, u32[]{:S(2)}) collective-permute-start(bf16[2,2,2,24,896]{4,3,0,1,2:T(8,128)(2,1)S(1)} %dynamic-slice_bitcast_fusion.12), channel_id=1, source_target_pairs={{0,2},{2,0},{1,3},{3,1},{4,6},{6,4},{5,7},{7,5},{8,10},{10,8},{9,1... | collective-permute-start | bytes 1032200 | tf_op jit(solution)/shard_map/ppermute | solution.py:242
  501.9 50.7 %collective-permute-start.45 = (bf16[2,2,2,96,768]{4,3,0,1,2:T(8,128)(2,1)}, bf16[2,2,2,96,768]{4,3,0,1,2:T(8,128)(2,1)}, u32[]{:S(2)}, u32[]{:S(2)}) collective-permute-start(bf16[2,2,2,96,768]{4,3,0,1,2:T(8,128)(2,1)} %dynamic-slice_bitcast_fusion.1), channel_id=1, source_target_pairs={{0,4},{4,0},{8,12},{12,8},{16,20},{20,16},{24,28},{28,24},{1,5},{5... | collective-permute-start | bytes 3538952 | tf_op jit(solution)/shard_map/ppermute | solution.py:242
  507.3 47.9 %collective-permute-start.40 = (bf16[2,2,2,24,3072]{4,3,0,1,2:T(8,128)(2,1)}, bf16[2,2,2,24,3072]{4,3,0,1,2:T(8,128)(2,1)}, u32[]{:S(2)}, u32[]{:S(2)}) collective-permute-start(bf16[2,2,2,24,3072]{4,3,0,1,2:T(8,128)(2,1)} %dynamic-slice_bitcast_fusion.2), channel_id=1, source_target_pairs={{0,2},{2,0},{1,3},{3,1},{4,6},{6,4},{5,7},{7,5},{8,10},{10,8},{9,1... | collective-permute-start | bytes 3538952 | tf_op jit(solution)/shard_map/ppermute | solution.py:242
  512.2 39.3 %collective-permute-start.24 = (bf16[512,768]{1,0:T(8,128)(2,1)S(1)}, bf16[512,768]{1,0:T(8,128)(2,1)}, u32[]{:S(2)}, u32[]{:S(2)}) collective-permute-start(bf16[512,768]{1,0:T(8,128)(2,1)S(1)} %fusion.33), channel_id=1, source_target_pairs={{0,2},{2,0},{1,3},{3,1},{4,6},{6,4},{5,7},{7,5},{8,10},{10,8},{9,1... | collective-permute-start | bytes 2359304 | tf_op jit(solution)/shard_map/ppermute | solution.py:242
  (96 other events, 930.2 us)

commit v2 on v1

--- a/solution.py
+++ b/solution.py
@@ -247,9 +247,9 @@
 
 
 def in_order(bit, mine, other, dim=0):
-    mine, other = jnp.expand_dims(mine, dim), jnp.expand_dims(other, dim)
-    place = lax.broadcasted_iota(jnp.int32, (1,) * dim + (2,) + (1,) * (mine.ndim - dim - 1), dim)
-    return jnp.where(place == bit, mine, other)
+    low = jnp.where(bit == 0, mine, other)
+    high = jnp.where(bit == 0, other, mine)
+    return jnp.stack([low, high], axis=dim)
 
 
 def grow(values, names):
@@ -328,16 +328,19 @@
     rank = lax.axis_index("y") // 2
     blocks = (2,) * len(wanted)
 
-    columns = jnp.concatenate(
-        [
-            query_bias, value_bias, output_bias, first_gain, first_shift, outer_bias, second_gain, second_shift,
-            inner_bias,
-        ]
-    )
-    used = columns.shape[0]
-    lines = -(-used // PAIR)
-    columns = jnp.pad(columns, (0, lines * PAIR - used)).reshape(lines, PAIR)
-    columns = jnp.pad(columns, ((0, own - lines), (0, 0)))
+    def in_rows(*vectors):
+        flat = jnp.concatenate(vectors)
+        lines = -(-flat.shape[0] // PAIR)
+        flat = jnp.pad(flat, (0, lines * PAIR - flat.shape[0])).reshape(lines, PAIR)
+        return jnp.pad(flat, ((0, own - lines), (0, 0)))
+
+    def from_rows(block, count):
+        lines = -(-count * own // PAIR)
+        flat = block.reshape(-1, own, PAIR)[:, :lines].reshape(-1, lines * PAIR).astype(f32)
+        return flat[:, : count * own]
+
+    columns = in_rows(query_bias, value_bias)
+    others = in_rows(output_bias, first_gain, first_shift, outer_bias, second_gain, second_shift, inner_bias)
 
     def three(index):
         return jnp.concatenate(
@@ -357,7 +360,7 @@
 
     attention_part = grow(attention_part, far)
     cut = (3 * half + PAIR) // 2 // 128 * 128
-    output_inner = jnp.concatenate([output_weight, inner_weight], axis=1)
+    output_inner = jnp.concatenate([output_weight, inner_weight, others], axis=1)
     output_inner, outer_part, attention_part = lax.optimization_barrier((output_inner, outer_weight, attention_part))
     part_a = grow(attention_part[..., :cut], [near] + y_names)
     part_b = grow(attention_part[..., cut:], y_names + [near])
@@ -365,21 +368,22 @@
     part_b = sort_blocks(part_b, far + y_names + [near], wanted).reshape(width, 3 * half + PAIR - cut)
     joined = jnp.concatenate([part_a, part_b], axis=1)
     qkv_weight = joined[:, : 3 * half]
-    vectors = joined[:, 3 * half :].reshape(-1, own, PAIR)[:, :lines].reshape(-1, lines * PAIR).astype(f32)
-    inner_bias = vectors[:, 8 * own : used].reshape(hidden)
-    vectors = vectors[:, : 8 * own].reshape(-1, 8, own).transpose(1, 0, 2).reshape(8, width)
+    vectors = from_rows(joined[:, 3 * half :], 2).reshape(-1, 2, own).transpose(1, 0, 2).reshape(2, width)
     half_of = lambda row: lax.dynamic_slice_in_dim(row, c * half, half, 0)
     qkv_bias = jnp.concatenate([half_of(vectors[0]), jnp.zeros((half,), f32), half_of(vectors[1])])
-    output_bias, first_gain, first_shift, outer_bias, second_gain, second_shift = [vectors[k] for k in range(2, 8)]
 
     output_inner = grow(output_inner, far)
     outer_part = grow(outer_part, far)
     output_inner = sort_blocks(grow(output_inner, [near] + y_names), far + [near] + y_names, wanted)
     outer_part = sort_blocks(grow(outer_part, y_names + [near]), far + y_names + [near], wanted)
-    output_inner = in_order(c, output_inner, swap(output_inner, core), len(wanted)).reshape(width, width + hidden)
+    output_inner = in_order(c, output_inner, swap(output_inner, core), len(wanted)).reshape(width, width + hidden + PAIR)
     outer_weight = in_order(c, outer_part, swap(outer_part, core), len(wanted)).reshape(hidden, width)
     output_weight = output_inner[:, :width]
-    inner_weight = output_inner[:, width:]
+    inner_weight = output_inner[:, width : width + hidden]
+    vectors = from_rows(output_inner[:, width + hidden :], 6 + chunks)
+    inner_bias = vectors[:, 6 * own :].reshape(hidden)
+    vectors = vectors[:, : 6 * own].reshape(-1, 6, own).transpose(1, 0, 2).reshape(6, width)
+    output_bias, first_gain, first_shift, outer_bias, second_gain, second_shift = [vectors[k] for k in range(6)]
 
     seg = pick(segments, y, 0)
     lo, hi = key_range(seg)
@@ -423,20 +427,19 @@
     d_second_shift = jnp.sum(grad, axis=0)
     d_outer = d_total.astype(bf16)
 
-    def core_then_chips(gradient, names):
+    def over_core(gradient):
         gradient = gradient.astype(bf16)
         rows, cols = gradient.shape
         shaped = gradient.reshape(blocks + (2, rows // (2 * math.prod(blocks)), cols))
         dim = len(wanted)
         got = swap(pick(shaped, 1 - c, dim), core)
-        summed = (pick(shaped, c, dim).astype(f32) + got.astype(f32)).astype(bf16)
-        return shrink(summed, names, wanted)
+        return (pick(shaped, c, dim).astype(f32) + got.astype(f32)).astype(bf16)
 
     back = list(reversed(far))
-    g_outer_weight = core_then_chips(dot_rows(active, d_outer), [near] + y_names + back)
+    g_outer_weight = shrink(over_core(dot_rows(active, d_outer)), [near] + y_names + back, wanted)
     d_inner = (dot_cols(d_outer, outer_weight) * slope.astype(f32)).astype(bf16)
     g_inner = dot_rows(first_low, d_inner)
-    g_inner_weight = core_then_chips(g_inner, y_names + [near] + back)
+    g_inner = over_core(g_inner)
     d_first = dot_cols(d_inner, inner_weight) + d_total
     d_pre = norm_back(d_first, first_gain, first_unit, first_inverse)
     d_attended = d_pre.astype(bf16)
@@ -462,7 +465,9 @@
     g_output = in_order(c, dot_rows(kept, d_attended).astype(bf16), dot_rows(got, d_attended).astype(bf16))
     g_output = g_output.reshape(width, width)
     g_columns = g_columns.astype(bf16)
-    g_output = core_then_chips(jnp.concatenate([g_output, g_columns], axis=1), y_names + [near] + back)
+    g_output = over_core(jnp.concatenate([g_output, g_columns], axis=1))
+    g_both = shrink(jnp.concatenate([g_inner, g_output], axis=-1), y_names + [near] + back, wanted)
+    g_inner_weight, g_output = g_both[:, :hidden], g_both[:, hidden:]
 
     part = attend_back(qkv, 0, steps // 2, (), mixed_all, d_heads, log_sums, seg_row, seg_col, lo, hi)
     rest = attend_back(

time: 598 us -> 556 us (0.930)
  local copies, waits for them, and re-layouts: 94.9 us -> 56.4 us
  other arithmetic: 90 us -> 59.2 us
  waiting for transfers between devices: 126 us -> 156 us
    select_n x29 -> x0, other arithmetic: 52.1 us -> none  [in_order(): return jnp.where(place == bit, mine, other)]
    broadcast_in_dim x23 -> x0, local copies, waits for them, and re-layouts: 34.2 us -> none  [in_order(): return jnp.where(place == bit, mine, other)]
    ppermute x49 -> x45, waiting for transfers between devices: 126 us -> 156 us  [swap(): return lax.ppermute(values, axis, [(i, i ^ step) for i in range(count)])]
    another operation x0 -> x41, other arithmetic: none -> 26.4 us  [in_order(): return jnp.stack([low, high], axis=dim)]
    concatenate x1, local copies, waits for them, and re-layouts: 6.1 us -> 0.1 us  [in_rows(): flat = jnp.concatenate(vectors)]
    unnamed x151 -> x128, local copies, waits for them, and re-layouts: 8.3 us -> 13.5 us
    ppermute x49 -> x45, starting transfers between devices: 67.8 us -> 63.8 us  [swap(): return lax.ppermute(values, axis, [(i, i ^ step) for i in range(count)])]
  transfers between devices with their start and end apart: 49 -> 45, of which waited for: 24 -> 21; matrix products, arithmetic and copies ran while one was open for 30% -> 20% of each run, Pallas kernels for 21% -> 23%
where the time goes in v2:
time: 556 us; the launch traced here: 549 us
  waiting for transfers between devices  156 us (28%)
  Pallas kernels  126 us (23%)
  matrix products  85.1 us (15%)
  starting transfers between devices  63.8 us (11%)
  other arithmetic  59.2 us (11%)
  local copies, waits for them, and re-layouts  56.4 us (10%)
    ppermute x45, waiting for transfers between devices, swap(): return lax.ppermute(values, axis, [(i, i ^ step) for i in range(count)])  156 us
    pallas_call x2, Pallas kernels, attend_back(): pl.pallas_call(functools.partial(attend_back_kernel, base=base, last=last...  73.1 us
    ppermute x45, starting transfers between devices, swap(): return lax.ppermute(values, axis, [(i, i ^ step) for i in range(count)])  63.8 us
    pallas_call x3, Pallas kernels, attend(): pl.pallas_call(functools.partial(attend_kernel, base=base), out_shape=(ja...  52.5 us
    dot_general x5, matrix products, dot(): return jnp.dot(left, right, preferred_element_type=f32)  32.1 us
    dot_general x6, matrix products, dot_cols(): lax.dot_general(left, right, (((1,), (1,)), ((), ())), preferred_element_...  29.3 us
    another operation x41, other arithmetic, in_order(): return jnp.stack([low, high], axis=dim)  26.4 us
    dot_general x5, matrix products, dot_rows(): lax.dot_general(left, right, (((0,), (0,)), ((), ())), preferred_element_...  23.7 us
  transfers between devices with their start and end apart: 45, of which 21 were waited for; matrix products, arithmetic and copies ran while one was open for 20% of the time, Pallas kernels for 23%

profile of v2, /device:TPU:0, one launch (start us, length us, event | category | flops | bytes accessed | tf_op | source)
XLA Modules:
  0.0 548.9 jit_solution(13672368620760063252)
XLA Ops:
  35.6 10.7 %collective-permute-done.9 = bf16[24,3968]{1,0:T(8,128)(2,1)S(1)} collective-permute-done((bf16[24,3968]{1,0:T(8,128)(2,1)S(1)}, bf16[24,3968]{1,0:T(8,128)(2,1)S(1)}, u32[]{:S(2)}, u32[]{:S(2)}) %collective-permute-start.9) | collective-permute-done | bytes 190496 | tf_op jit(solution)/shard_map/ppermute | solution.py:242
  67.1 7.5 %collective-permute-done.17 = bf16[2,2,96,768]{3,2,0,1:T(8,128)(2,1)S(1)} collective-permute-done((bf16[2,2,96,768]{3,2,0,1:T(8,128)(2,1)S(1)}, bf16[2,2,96,768]{3,2,0,1:T(8,128)(2,1)S(1)}, u32[]{:S(2)}, u32[]{:S(2)}) %collective-permute-start.17) | collective-permute-done | bytes 589856 | tf_op jit(solution)/shard_map/ppermute | solution.py:242
  86.0 18.8 %collective-permute-done.18 = bf16[2,2,2,96,768]{4,3,0,1,2:T(8,128)(2,1)} collective-permute-done((bf16[2,2,2,96,768]{4,3,0,1,2:T(8,128)(2,1)}, bf16[2,2,2,96,768]{4,3,0,1,2:T(8,128)(2,1)}, u32[]{:S(2)}, u32[]{:S(2)}) %collective-permute-start.18) | collective-permute-done | bytes 1179680 | tf_op jit(solution)/shard_map/ppermute | solution.py:242
  106.3 6.8 %collective-permute-done.12 = bf16[2,2,2,24,3968]{4,3,0,1,2:T(8,128)(2,1)} collective-permute-done((bf16[2,2,2,24,3968]{4,3,0,1,2:T(8,128)(2,1)S(1)}, bf16[2,2,2,24,3968]{4,3,0,1,2:T(8,128)(2,1)}, u32[]{:S(2)}, u32[]{:S(2)}) %collective-permute-start.12) | collective-permute-done | bytes 1523744 | tf_op jit(solution)/shard_map/ppermute | solution.py:242
  121.7 6.4 %add_convert_fusion.q_ref.k_ref.v_ref = bf16[2048,1152]{1,0:T(8,128)(2,1)} fusion(bf16[2048,768]{1,0:T(8,128)(2,1)S(1)} %bitcast.404, f32[1152]{0:T(1024)S(1)} %pad_maximum_fusion.30, bf16[768,640]{1,0:T(8,128)(2,1)S(1)} %bitcast.430, bf16[768,640]{1,0:T(8,128)(2,1)S(1)} %bitcast.433), kind=kOutput, calls=%fused_computation.9 | convolution fusion | flops 3632136192 | bytes 9835008 | tf_op jit(solution)/shard_map/dot_general | solution.py:26
  130.1 19.9 %attend.4 = (bf16[768,384]{1,0:T(8,128)(2,1)}, f32[48,768]{1,0:T(8,128)}) custom-call(s32[8]{0:T(128)} %get-tuple-element.173.lo, s32[8]{0:T(128)} %get-tuple-element.172.hi, bf16[2048,1152]{1,0:T(8,128)(2,1)} %add_convert_fusion.q_ref.k_ref.v_ref, bf16[2048,1152]{1,0:T(8,128)(2,1)} %add_convert_fusion.q_ref.k_ref.v_ref, ...), custom_call_target="tpu_custom_call" | custom-call | tf_op jit(solution)/shard_map/attend/pallas_call | solution.py:168
  150.0 17.7 %attend.3 = (bf16[768,384]{1,0:T(8,128)(2,1)}, f32[48,768]{1,0:T(8,128)}) custom-call(s32[8]{0:T(128)} %get-tuple-element.173.lo, s32[8]{0:T(128)} %get-tuple-element.172.hi, bf16[2048,1152]{1,0:T(8,128)(2,1)} %add_convert_fusion.q_ref.k_ref.v_ref, bf16[2048,1152]{1,0:T(8,128)(2,1)} %add_convert_fusion.q_ref.k_ref.v_ref, ...), custom_call_target="tpu_custom_call" | custom-call | tf_op jit(solution)/shard_map/attend/pallas_call | solution.py:168
  167.7 15.0 %attend.5 = (bf16[512,384]{1,0:T(8,128)(2,1)}, f32[48,512]{1,0:T(8,128)}) custom-call(s32[8]{0:T(128)} %get-tuple-element.173.lo, s32[8]{0:T(128)} %get-tuple-element.172.hi, bf16[2048,1152]{1,0:T(8,128)(2,1)} %add_convert_fusion.q_ref.k_ref.v_ref, bf16[2048,1152]{1,0:T(8,128)(2,1)} %add_convert_fusion.q_ref.k_ref.v_ref, ...), custom_call_target="tpu_custom_call" | custom-call | tf_op jit(solution)/shard_map/attend/pallas_call | solution.py:168
  211.5 10.7 %multiply_convert_fusion.1 = (bf16[1024,3072]{1,0:T(8,128)(2,1)S(1)}, f32[1024,3072]{1,0:T(8,128)}) fusion(f32[3072]{0:T(1024)S(1)} %add.370, bf16[768,3968]{1,0:T(8,128)(2,1)} %bitcast.410, f32[1024,768]{1,0:T(8,128)S(1)} %get-tuple-element.164, f32[768]{0:T(1024)S(1)} %add.367, f32[768]{0:T(1024)S(1)} %mul.156, f32[1024]{0:T(1024)S(1)} %add_rsqrt_fusion.1, ...), kind=kOutput, calls=%fused_computation.7 | convolution fusion | flops 4854644736 | bytes 26765312 | tf_op jit(solution)/shard_map/dot_general | solution.py:26
  222.2 11.0 %fusion.91 = (f32[1024]{0:T(1024)S(1)}, f32[1024,768]{1,0:T(8,128)S(1)}) fusion(f32[768]{0:T(1024)S(1)} %add.376, bf16[1024,3072]{1,0:T(8,128)(2,1)S(1)} %get-tuple-element.165, bf16[3072,768]{1,0:T(8,128)(2,1)} %bitcast.416, f32[768]{0:T(1024)S(1)} %add.367, f32[768]{0:T(1024)S(1)} %mul.156, f32[1024]{0:T(1024)S(1)} %add_rsqrt_fusion.1, ...), kind=kOutput, calls=%fused_computation.322 | convolution fusion | flops 4837342208 | bytes 17323008 | tf_op jit(solution)/shard_map/dot_general | solution.py:26
  241.2 5.7 %convolution_convert_fusion = bf16[3072,768]{1,0:T(8,128)(2,1)S(1)} fusion(bf16[1024,3072]{1,0:T(8,128)(2,1)S(1)} %copy-done.54, f32[1024,768]{1,0:T(8,128)S(1)} %get-tuple-element.68), kind=kOutput, calls=%fused_computation.11 | convolution fusion | flops 4834983936 | bytes 14155776 | tf_op jit(solution)/shard_map/dot_general | solution.py:298
  247.0 13.7 %fusion.92 = (bf16[3072]{0:T(1024)(128)(2,1)S(1)}, bf16[1024,3072]{1,0:T(8,128)(2,1)}) fusion(f32[1024,3072]{1,0:T(8,128)} %get-tuple-element.166, f32[3072]{0:T(1024)S(1)} %add.370, bf16[3072,768]{1,0:T(8,128)(2,1)S(1)} %bitcast.419, f32[1024,768]{1,0:T(8,128)S(1)} %get-tuple-element.68), kind=kOutput, calls=%fused_computation.323 | convolution fusion | flops 4876661760 | bytes 26757120 | tf_op jit(solution)/shard_map/dot_general | solution.py:302
  260.7 8.2 %multiply_reduce_fusion = (bf16[768]{0:T(1024)(128)(2,1)S(1)}, f32[1024]{0:T(1024)S(1)}, f32[1024]{0:T(1024)S(1)}, bf16[768]{0:T(1024)(128)(2,1)S(1)}, f32[1024,768]{1,0:T(8,128)S(1)}) fusion(f32[1024,768]{1,0:T(8,128)S(1)} %copy-done.1, f32[1024]{0:T(1024)S(1)} %add_rsqrt_fusion.1, f32[1024]{0:T(1024)S(1)} %broadcast_multiply_fusion.4, f32[768]{0:T(1024)S(1)} %mul.156, ...), kind=kOutput, calls=%fused_computation.43 | convolution fusion | flops 4839698432 | bytes 20470784 | tf_op jit(solution)/shard_map/dot_general | solution.py:302
  268.9 9.9 %convolution_convert_fusion.1 = bf16[768,3072]{1,0:T(8,128)(2,1)} fusion(bf16[1024,3072]{1,0:T(8,128)(2,1)} %get-tuple-element.171, f32[1024,768]{1,0:T(8,128)S(1)} %copy-done.1, f32[768]{0:T(1024)S(1)} %add.367, f32[768]{0:T(1024)S(1)} %mul.156, f32[1024]{0:T(1024)S(1)} %add_rsqrt_fusion.1, f32[1024]{0:T(1024)S(1)} %broadcast_multiply_fusion.4), kind=kOutput, calls=%fused_computation.12 | convolution fusion | flops 4838129664 | bytes 14170112 | tf_op jit(solution)/shard_map/dot_general | solution.py:298
  310.9 32.1 %attend_back.2 = (bf16[1024,384]{1,0:T(8,128)(2,1)}, f32[2048,384]{1,0:T(8,128)}, f32[2048,384]{1,0:T(8,128)}) custom-call(s32[8]{0:T(128)} %get-tuple-element.173.lo, s32[8]{0:T(128)} %get-tuple-element.172.hi, bf16[2048,1152]{1,0:T(8,128)(2,1)} %add_convert_fusion.q_ref.k_ref.v_ref, bf16[2048,1152]{1,0:T(8,128)(2,1)} %add_convert_fusion.q_ref.k_ref.v_ref, ...), custom_call_target="tpu_custom_call" | custom-call | tf_op jit(solution)/shard_map/attend_back/pallas_call | solution.py:205
  344.3 41.0 %attend_back.3 = (bf16[1024,384]{1,0:T(8,128)(2,1)}, bf16[2048,384]{1,0:T(8,128)(2,1)}, bf16[2048,384]{1,0:T(8,128)(2,1)}) custom-call(s32[8]{0:T(128)} %get-tuple-element.173.lo, s32[8]{0:T(128)} %get-tuple-element.172.hi, bf16[2048,1152]{1,0:T(8,128)(2,1)} %add_convert_fusion.q_ref.k_ref.v_ref, bf16[2048,1152]{1,0:T(8,128)(2,1)} %add_convert_fusion.q_ref.k_ref.v_ref, ...), custom_call_target="tpu_custom_call" | custom-call | tf_op jit(solution)/shard_map/attend_back/pallas_call | solution.py:205
  420.2 9.2 %collective-permute-start.27 = (bf16[2,48,640]{2,1,0:T(8,128)(2,1)S(1)}, bf16[2,48,640]{2,1,0:T(8,128)(2,1)S(1)}, u32[]{:S(2)}, u32[]{:S(2)}) collective-permute-start(bf16[2,48,640]{2,1,0:T(8,128)(2,1)S(1)} %dynamic-slice_bitcast_fusion.16), channel_id=1, source_target_pairs={{0,8},{4,12},{8,0},{12,4},{16,24},{20,28},{24,16},{28,20},{1,9},{5... | collective-permute-start | bytes 368648 | tf_op jit(solution)/shard_map/ppermute | solution.py:242
  456.7 19.3 %collective-permute-done.41 = bf16[2,2,2,96,768]{4,3,0,1,2:T(8,128)(2,1)S(1)} collective-permute-done((bf16[2,2,2,96,768]{4,3,0,1,2:T(8,128)(2,1)S(1)}, bf16[2,2,2,96,768]{4,3,0,1,2:T(8,128)(2,1)S(1)}, u32[]{:S(2)}, u32[]{:S(2)}) %collective-permute-start.41) | collective-permute-done | bytes 1179680 | tf_op jit(solution)/shard_map/ppermute | solution.py:242
  477.3 10.6 %collective-permute-done.36 = bf16[2,2,2,24,3968]{4,3,0,1,2:T(8,128)(2,1)S(1)} collective-permute-done((bf16[2,2,2,24,3968]{4,3,0,1,2:T(8,128)(2,1)S(1)}, bf16[2,2,2,24,3968]{4,3,0,1,2:T(8,128)(2,1)S(1)}, u32[]{:S(2)}, u32[]{:S(2)}) %collective-permute-start.36) | collective-permute-done | bytes 1523744 | tf_op jit(solution)/shard_map/ppermute | solution.py:242
  490.0 14.7 %collective-permute-done.24 = bf16[512,768]{1,0:T(8,128)(2,1)S(1)} collective-permute-done((bf16[512,768]{1,0:T(8,128)(2,1)S(1)}, bf16[512,768]{1,0:T(8,128)(2,1)S(1)}, u32[]{:S(2)}, u32[]{:S(2)}) %collective-permute-start.24) | collective-permute-done | bytes 786464 | tf_op jit(solution)/shard_map/ppermute | solution.py:242
  505.0 11.6 %collective-permute-done.42 = bf16[2,2,96,768]{3,2,0,1:T(8,128)(2,1)S(1)} collective-permute-done((bf16[2,2,96,768]{3,2,0,1:T(8,128)(2,1)S(1)}, bf16[2,2,96,768]{3,2,0,1:T(8,128)(2,1)S(1)}, u32[]{:S(2)}, u32[]{:S(2)}) %collective-permute-start.42) | collective-permute-done | bytes 589856 | tf_op jit(solution)/shard_map/ppermute | solution.py:242
  521.0 5.7 %collective-permute-done.43 = bf16[2,96,768]{2,1,0:T(8,128)(2,1)S(1)} collective-permute-done((bf16[2,96,768]{2,1,0:T(8,128)(2,1)S(1)}, bf16[2,96,768]{2,1,0:T(8,128)(2,1)S(1)}, u32[]{:S(2)}, u32[]{:S(2)}) %collective-permute-start.43) | collective-permute-done | bytes 294944 | tf_op jit(solution)/shard_map/ppermute | solution.py:242
  528.7 7.7 %collective-permute-done.38 = bf16[2,24,3968]{2,1,0:T(8,128)(2,1)S(1)} collective-permute-done((bf16[2,24,3968]{2,1,0:T(8,128)(2,1)S(1)}, bf16[2,24,3968]{2,1,0:T(8,128)(2,1)S(1)}, u32[]{:S(2)}, u32[]{:S(2)}) %collective-permute-start.38) | collective-permute-done | bytes 380960 | tf_op jit(solution)/shard_map/ppermute | solution.py:242
  537.6 8.2 %collective-permute-done.39 = bf16[24,3968]{1,0:T(8,128)(2,1)S(1)} collective-permute-done((bf16[24,3968]{1,0:T(8,128)(2,1)S(1)}, bf16[24,3968]{1,0:T(8,128)(2,1)S(1)}, u32[]{:S(2)}, u32[]{:S(2)}) %collective-permute-start.39) | collective-permute-done | bytes 190496 | tf_op jit(solution)/shard_map/ppermute | solution.py:242
  (411 shorter events, 224.2 us)
Async XLA Ops:
  4.9 46.1 %collective-permute-start = (bf16[512,768]{1,0:T(8,128)(2,1)S(1)}, bf16[512,768]{1,0:T(8,128)(2,1)}, u32[]{:S(2)}, u32[]{:S(2)}) collective-permute-start(bf16[512,768]{1,0:T(8,128)(2,1)S(1)} %dynamic-slice_bitcast_fusion.4), channel_id=1, source_target_pairs={{0,2},{2,0},{1,3},{3,1},{4,6},{6,4},{5,7},{7,5},{8,10},{10,8},{9,1... | collective-permute-start | bytes 2359304 | tf_op jit(solution)/shard_map/ppermute | solution.py:242
  8.7 55.9 %collective-permute-start.21 = (bf16[512,768]{1,0:T(8,128)(2,1)S(1)}, bf16[512,768]{1,0:T(8,128)(2,1)S(1)}, u32[]{:S(2)}, u32[]{:S(2)}) collective-permute-start(bf16[512,768]{1,0:T(8,128)(2,1)S(1)} %dynamic-slice_bitcast_fusion.1), channel_id=1, source_target_pairs={{0,2},{2,0},{1,3},{3,1},{4,6},{6,4},{5,7},{7,5},{8,10},{10,8},{9,1... | collective-permute-start | bytes 2359304 | tf_op jit(solution)/shard_map/ppermute | solution.py:242
  28.8 17.5 %collective-permute-start.5 = (bf16[2,2,48,640]{3,2,0,1:T(8,128)(2,1)S(1)}, bf16[2,2,48,640]{3,2,0,1:T(8,128)(2,1)S(1)}, u32[]{:S(2)}, u32[]{:S(2)}) collective-permute-start(bf16[2,2,48,640]{3,2,0,1:T(8,128)(2,1)S(1)} %get-tuple-element.127), channel_id=1, source_target_pairs={{0,4},{4,0},{8,12},{12,8},{16,20},{20,16},{24,28},{28,24},{1,5},{5... | collective-permute-start | bytes 737288 | tf_op jit(solution)/shard_map/ppermute | solution.py:242
  30.4 18.1 %collective-permute-start.7 = (bf16[2,2,48,640]{3,2,0,1:T(8,128)(2,1)S(1)}, bf16[2,2,48,640]{3,2,0,1:T(8,128)(2,1)S(1)}, u32[]{:S(2)}, u32[]{:S(2)}) collective-permute-start(bf16[2,2,48,640]{3,2,0,1:T(8,128)(2,1)S(1)} %get-tuple-element.128), channel_id=1, source_target_pairs={{0,2},{2,0},{1,3},{3,1},{4,6},{6,4},{5,7},{7,5},{8,10},{10,8},{9,1... | collective-permute-start | bytes 737288 | tf_op jit(solution)/shard_map/ppermute | solution.py:242
  49.4 35.3 %collective-permute-start.6 = (bf16[2,2,2,48,640]{4,3,0,1,2:T(8,128)(2,1)}, bf16[2,2,2,48,640]{4,3,0,1,2:T(8,128)(2,1)}, u32[]{:S(2)}, u32[]{:S(2)}) collective-permute-start(bf16[2,2,2,48,640]{4,3,0,1,2:T(8,128)(2,1)} %pad_maximum_fusion.17), channel_id=1, source_target_pairs={{0,2},{2,0},{1,3},{3,1},{4,6},{6,4},{5,7},{7,5},{8,10},{10,8},{9,1... | collective-permute-start | bytes 1474568 | tf_op jit(solution)/shard_map/ppermute | solution.py:242
  51.0 31.2 %collective-permute-start.8 = (bf16[2,2,2,48,640]{4,3,1,2,0:T(8,128)(2,1)S(1)}, bf16[2,2,2,48,640]{4,3,1,2,0:T(8,128)(2,1)S(1)}, u32[]{:S(2)}, u32[]{:S(2)}) collective-permute-start(bf16[2,2,2,48,640]{4,3,1,2,0:T(8,128)(2,1)S(1)} %pad_maximum_fusion.18), channel_id=1, source_target_pairs={{0,4},{4,0},{8,12},{12,8},{16,20},{20,16},{24,28},{28,24},{1,5},{5... | collective-permute-start | bytes 1474568 | tf_op jit(solution)/shard_map/ppermute | solution.py:242
  56.3 18.4 %collective-permute-start.17 = (bf16[2,2,96,768]{3,2,0,1:T(8,128)(2,1)S(1)}, bf16[2,2,96,768]{3,2,0,1:T(8,128)(2,1)S(1)}, u32[]{:S(2)}, u32[]{:S(2)}) collective-permute-start(bf16[2,2,96,768]{3,2,0,1:T(8,128)(2,1)S(1)} %pad_maximum_fusion.15), channel_id=1, source_target_pairs={{0,2},{2,0},{1,3},{3,1},{4,6},{6,4},{5,7},{7,5},{8,10},{10,8},{9,1... | collective-permute-start | bytes 1769480 | tf_op jit(solution)/shard_map/ppermute | solution.py:242
  61.8 20.0 %collective-permute-start.11 = (bf16[2,2,24,3968]{3,2,0,1:T(8,128)(2,1)S(1)}, bf16[2,2,24,3968]{3,2,0,1:T(8,128)(2,1)S(1)}, u32[]{:S(2)}, u32[]{:S(2)}) collective-permute-start(bf16[2,2,24,3968]{3,2,0,1:T(8,128)(2,1)S(1)} %pad_maximum_fusion.14), channel_id=1, source_target_pairs={{0,4},{4,0},{8,12},{12,8},{16,20},{20,16},{24,28},{28,24},{1,5},{5... | collective-permute-start | bytes 2285576 | tf_op jit(solution)/shard_map/ppermute | solution.py:242
  64.7 54.2 %collective-permute-start.1 = (bf16[2,512,768]{2,1,0:T(8,128)(2,1)}, bf16[2,512,768]{2,1,0:T(8,128)(2,1)}, u32[]{:S(2)}, u32[]{:S(2)}) collective-permute-start(bf16[2,512,768]{2,1,0:T(8,128)(2,1)} %pad_maximum_fusion.6), channel_id=1, source_target_pairs={{0,1},{1,0},{2,3},{3,2},{4,5},{5,4},{6,7},{7,6},{8,9},{9,8},{10,11... | collective-permute-start | bytes 4718600 | tf_op jit(solution)/shard_map/ppermute | solution.py:242
  75.9 29.0 %collective-permute-start.18 = (bf16[2,2,2,96,768]{4,3,0,1,2:T(8,128)(2,1)}, bf16[2,2,2,96,768]{4,3,0,1,2:T(8,128)(2,1)}, u32[]{:S(2)}, u32[]{:S(2)}) collective-permute-start(bf16[2,2,2,96,768]{4,3,0,1,2:T(8,128)(2,1)} %pad_maximum_fusion.12), channel_id=1, source_target_pairs={{0,4},{4,0},{8,12},{12,8},{16,20},{20,16},{24,28},{28,24},{1,5},{5... | collective-permute-start | bytes 3538952 | tf_op jit(solution)/shard_map/ppermute | solution.py:242
  82.1 31.0 %collective-permute-start.12 = (bf16[2,2,2,24,3968]{4,3,0,1,2:T(8,128)(2,1)S(1)}, bf16[2,2,2,24,3968]{4,3,0,1,2:T(8,128)(2,1)}, u32[]{:S(2)}, u32[]{:S(2)}) collective-permute-start(bf16[2,2,2,24,3968]{4,3,0,1,2:T(8,128)(2,1)S(1)} %pad_maximum_fusion.10), channel_id=1, source_target_pairs={{0,2},{2,0},{1,3},{3,1},{4,6},{6,4},{5,7},{7,5},{8,10},{10,8},{9,1... | collective-permute-start | bytes 4571144 | tf_op jit(solution)/shard_map/ppermute | solution.py:242
  116.7 83.8 %collective-permute-start.13 = (bf16[2,2,2,2,24,3968]{5,4,3,2,1,0:T(8,128)(2,1)}, bf16[2,2,2,2,24,3968]{5,4,3,2,1,0:T(8,128)(2,1)}, u32[]{:S(2)}, u32[]{:S(2)}) collective-permute-start(bf16[2,2,2,2,24,3968]{5,4,3,2,1,0:T(8,128)(2,1)} %maximum_bitcast_fusion), channel_id=1, source_target_pairs={{0,1},{1,0},{2,3},{3,2},{4,5},{5,4},{6,7},{7,6},{8,9},{9,8},{10,11... | collective-permute-start | bytes 9142280 | tf_op jit(solution)/shard_map/ppermute | solution.py:242
  118.3 76.8 %collective-permute-start.19 = (bf16[2,2,2,2,96,768]{5,4,3,2,1,0:T(8,128)(2,1)}, bf16[2,2,2,2,96,768]{5,4,3,2,1,0:T(8,128)(2,1)}, u32[]{:S(2)}, u32[]{:S(2)}) collective-permute-start(bf16[2,2,2,2,96,768]{5,4,3,2,1,0:T(8,128)(2,1)} %maximum_bitcast_fusion.1), channel_id=1, source_target_pairs={{0,1},{1,0},{2,3},{3,2},{4,5},{5,4},{6,7},{7,6},{8,9},{9,8},{10,11... | collective-permute-start | bytes 7077896 | tf_op jit(solution)/shard_map/ppermute | solution.py:242
  188.4 18.9 %collective-permute-start.14 = (bf16[2,512,384]{2,1,0:T(8,128)(2,1)}, bf16[2,512,384]{2,1,0:T(8,128)(2,1)}, u32[]{:S(2)}, u32[]{:S(2)}) collective-permute-start(bf16[2,512,384]{2,1,0:T(8,128)(2,1)} %get-tuple-element.101), channel_id=1, source_target_pairs={{0,1},{1,0},{2,3},{3,2},{4,5},{5,4},{6,7},{7,6},{8,9},{9,8},{10,11... | collective-permute-start | bytes 2359304 | tf_op jit(solution)/shard_map/ppermute | solution.py:242
  287.3 157.7 %collective-permute-start.40 = (bf16[2,2,2,2,96,768]{5,4,0,1,3,2:T(8,128)(2,1)}, bf16[2,2,2,2,96,768]{5,4,0,1,3,2:T(8,128)(2,1)}, u32[]{:S(2)}, u32[]{:S(2)}) collective-permute-start(bf16[2,2,2,2,96,768]{5,4,0,1,3,2:T(8,128)(2,1)} %bitcast.394), channel_id=1, source_target_pairs={{0,1},{1,0},{2,3},{3,2},{4,5},{5,4},{6,7},{7,6},{8,9},{9,8},{10,11... | collective-permute-start | bytes 7077896 | tf_op jit(solution)/shard_map/ppermute | solution.py:242
  305.6 143.3 %collective-permute-start.34 = (bf16[2,2,2,2,24,3072]{5,4,0,1,2,3:T(8,128)(2,1)}, bf16[2,2,2,2,24,3072]{5,4,0,1,2,3:T(8,128)(2,1)}, u32[]{:S(2)}, u32[]{:S(2)}) collective-permute-start(bf16[2,2,2,2,24,3072]{5,4,0,1,2,3:T(8,128)(2,1)} %bitcast.395), channel_id=1, source_target_pairs={{0,1},{1,0},{2,3},{3,2},{4,5},{5,4},{6,7},{7,6},{8,9},{9,8},{10,11... | collective-permute-start | bytes 7077896 | tf_op jit(solution)/shard_map/ppermute | solution.py:242
  307.1 101.3 %collective-permute-start.20 = (bf16[512,768]{1,0:T(8,128)(2,1)}, bf16[512,768]{1,0:T(8,128)(2,1)}, u32[]{:S(2)}, u32[]{:S(2)}) collective-permute-start(bf16[512,768]{1,0:T(8,128)(2,1)} %dynamic-slice_bitcast_fusion.2), channel_id=1, source_target_pairs={{0,2},{2,0},{1,3},{3,1},{4,6},{6,4},{5,7},{7,5},{8,10},{10,8},{9,1... | collective-permute-start | bytes 2359304 | tf_op jit(solution)/shard_map/ppermute | solution.py:242
  408.4 44.8 %collective-permute-start.23 = (bf16[1024,768]{1,0:T(8,128)(2,1)S(1)}, bf16[1024,768]{1,0:T(8,128)(2,1)S(1)}, u32[]{:S(2)}, u32[]{:S(2)}) collective-permute-start(bf16[1024,768]{1,0:T(8,128)(2,1)S(1)} %convolution_convert_fusion.2), channel_id=1, source_target_pairs={{0,1},{1,0},{2,3},{3,2},{4,5},{5,4},{6,7},{7,6},{8,9},{9,8},{10,11... | collective-permute-start | bytes 4718600 | tf_op jit(solution)/shard_map/ppermute | solution.py:242
  447.7 28.4 %collective-permute-start.41 = (bf16[2,2,2,96,768]{4,3,0,1,2:T(8,128)(2,1)S(1)}, bf16[2,2,2,96,768]{4,3,0,1,2:T(8,128)(2,1)S(1)}, u32[]{:S(2)}, u32[]{:S(2)}) collective-permute-start(bf16[2,2,2,96,768]{4,3,0,1,2:T(8,128)(2,1)S(1)} %dynamic-slice_bitcast_fusion), channel_id=1, source_target_pairs={{0,4},{4,0},{8,12},{12,8},{16,20},{20,16},{24,28},{28,24},{1,5},{5... | collective-permute-start | bytes 3538952 | tf_op jit(solution)/shard_map/ppermute | solution.py:242
  451.6 36.3 %collective-permute-start.36 = (bf16[2,2,2,24,3968]{4,3,0,1,2:T(8,128)(2,1)S(1)}, bf16[2,2,2,24,3968]{4,3,0,1,2:T(8,128)(2,1)S(1)}, u32[]{:S(2)}, u32[]{:S(2)}) collective-permute-start(bf16[2,2,2,24,3968]{4,3,0,1,2:T(8,128)(2,1)S(1)} %fusion.34), channel_id=1, source_target_pairs={{0,2},{2,0},{1,3},{3,1},{4,6},{6,4},{5,7},{7,5},{8,10},{10,8},{9,1... | collective-permute-start | bytes 4571144 | tf_op jit(solution)/shard_map/ppermute | solution.py:242
  455.7 49.0 %collective-permute-start.24 = (bf16[512,768]{1,0:T(8,128)(2,1)S(1)}, bf16[512,768]{1,0:T(8,128)(2,1)S(1)}, u32[]{:S(2)}, u32[]{:S(2)}) collective-permute-start(bf16[512,768]{1,0:T(8,128)(2,1)S(1)} %fusion.42), channel_id=1, source_target_pairs={{0,2},{2,0},{1,3},{3,1},{4,6},{6,4},{5,7},{7,5},{8,10},{10,8},{9,1... | collective-permute-start | bytes 2359304 | tf_op jit(solution)/shard_map/ppermute | solution.py:242
  476.4 40.2 %collective-permute-start.42 = (bf16[2,2,96,768]{3,2,0,1:T(8,128)(2,1)S(1)}, bf16[2,2,96,768]{3,2,0,1:T(8,128)(2,1)S(1)}, u32[]{:S(2)}, u32[]{:S(2)}) collective-permute-start(bf16[2,2,96,768]{3,2,0,1:T(8,128)(2,1)S(1)} %dynamic-slice_bitcast_fusion.6), channel_id=1, source_target_pairs={{0,2},{2,0},{1,3},{3,1},{4,6},{6,4},{5,7},{7,5},{8,10},{10,8},{9,1... | collective-permute-start | bytes 1769480 | tf_op jit(solution)/shard_map/ppermute | solution.py:242
  488.3 28.5 %collective-permute-start.37 = (bf16[2,2,24,3968]{3,2,0,1:T(8,128)(2,1)S(1)}, bf16[2,2,24,3968]{3,2,0,1:T(8,128)(2,1)S(1)}, u32[]{:S(2)}, u32[]{:S(2)}) collective-permute-start(bf16[2,2,24,3968]{3,2,0,1:T(8,128)(2,1)S(1)} %dynamic-slice_bitcast_fusion.5), channel_id=1, source_target_pairs={{0,4},{4,0},{8,12},{12,8},{16,20},{20,16},{24,28},{28,24},{1,5},{5... | collective-permute-start | bytes 2285576 | tf_op jit(solution)/shard_map/ppermute | solution.py:242
  517.1 19.3 %collective-permute-start.38 = (bf16[2,24,3968]{2,1,0:T(8,128)(2,1)S(1)}, bf16[2,24,3968]{2,1,0:T(8,128)(2,1)S(1)}, u32[]{:S(2)}, u32[]{:S(2)}) collective-permute-start(bf16[2,24,3968]{2,1,0:T(8,128)(2,1)S(1)} %dynamic-slice_bitcast_fusion.7), channel_id=1, source_target_pairs={{0,8},{4,12},{8,0},{12,4},{16,24},{20,28},{24,16},{28,20},{1,9},{5... | collective-permute-start | bytes 1142792 | tf_op jit(solution)/shard_map/ppermute | solution.py:242
  (80 other events, 663.2 us)
